TPU v7x, 32 devices: a whole 2x2x4 slice. The times are simulated.
32 devices in a mesh: wide: 8 (over z, x), narrow: 4 (over y, core).
Axes of the slice: x: 2, y: 2, z: 4, core: 2. Of those that a mesh axis runs over, the one named last changes fastest.
Arguments:
- tokens: bfloat16 [16384, 768], P(('wide', 'narrow')), may hold values from -6 to 6
- cotangent: bfloat16 [16384, 768], P(('wide', 'narrow')), may hold values from -6 to 6
- segments: int32 [32, 512], P(('wide', 'narrow')), may hold values from 0 to 3, never falling along the last dimension, each value on 1 to 256 neighbouring positions
- buckets: int32 [512, 512], replicated, may hold values from 0 to 255
- norm1_gain: bfloat16 [768], P(('wide', 'narrow')), may hold values from 0.099609375 to 1.8984375
- norm1_bias: bfloat16 [768], P(('wide', 'narrow')), may hold values from -3 to 3
- qkv_weight: bfloat16 [768, 2304], P(('wide', 'narrow')), may hold values from -0.21875 to 0.21875
- qv_bias: bfloat16 [1536], P(('wide', 'narrow')), may hold values from -3 to 3
- head_scale: bfloat16 [12], replicated, may hold values from 0.5 to 2
- rel_table: bfloat16 [256, 12], P(('wide', 'narrow')), may hold values from -4 to 4
- out_weight: bfloat16 [768, 768], P(('wide', 'narrow')), may hold values from -0.21875 to 0.21875
- out_bias: bfloat16 [768], P(('wide', 'narrow')), may hold values from -3 to 3
- post_gain: bfloat16 [768], P(('wide', 'narrow')), may hold values from 0.099609375 to 1.8984375
- post_bias: bfloat16 [768], P(('wide', 'narrow')), may hold values from -3 to 3
- norm2_gain: bfloat16 [768], P(('wide', 'narrow')), may hold values from 0.099609375 to 1.8984375
- norm2_bias: bfloat16 [768], P(('wide', 'narrow')), may hold values from -3 to 3
- fc1_weight: bfloat16 [768, 3072], P(('wide', 'narrow')), may hold values from -0.21875 to 0.21875
- fc1_bias: bfloat16 [3072], P(('wide', 'narrow')), may hold values from -3 to 3
- inner_gain: bfloat16 [3072], P(('wide', 'narrow')), may hold values from 0.099609375 to 1.8984375
- inner_bias: bfloat16 [3072], P(('wide', 'narrow')), may hold values from -3 to 3
- fc2_weight: bfloat16 [3072, 768], P(('wide', 'narrow')), may hold values from -0.109375 to 0.109375
- fc2_bias: bfloat16 [768], P(('wide', 'narrow')), may hold values from -3 to 3
Outputs:
- output: bfloat16 [16384, 768], P(('wide', 'narrow'))
- grad_tokens: bfloat16 [16384, 768], P(('wide', 'narrow'))
- grad_norm1_gain: float32 [768], P(('wide', 'narrow'))
- grad_norm1_bias: float32 [768], P(('wide', 'narrow'))
- grad_qkv_weight: float32 [768, 2304], P(('wide', 'narrow'))
- grad_qv_bias: float32 [1536], P(('wide', 'narrow'))
- grad_head_scale: float32 [12], replicated
- grad_rel_table: float32 [256, 12], P(('wide', 'narrow'))
- grad_out_weight: float32 [768, 768], P(('wide', 'narrow'))
- grad_out_bias: float32 [768], P(('wide', 'narrow'))
- grad_post_gain: float32 [768], P(('wide', 'narrow'))
- grad_post_bias: float32 [768], P(('wide', 'narrow'))
- grad_norm2_gain: float32 [768], P(('wide', 'narrow'))
- grad_norm2_bias: float32 [768], P(('wide', 'narrow'))
- grad_fc1_weight: float32 [768, 3072], P(('wide', 'narrow'))
- grad_fc1_bias: float32 [3072], P(('wide', 'narrow'))
- grad_inner_gain: float32 [3072], P(('wide', 'narrow'))
- grad_inner_bias: float32 [3072], P(('wide', 'narrow'))
- grad_fc2_weight: float32 [3072, 768], P(('wide', 'narrow'))
- grad_fc2_bias: float32 [768], P(('wide', 'narrow'))
Inputs may be any that keep to these rules, and one draw needn't show every extreme that they name: `segments`: segment numbers never fall along a row; each document has at most 256 tokens.
All inputs are finite; a program needn't handle non-finite values.
Results may differ from a plain program's by a relative error of at most 0.012.
Values may be sent and summed in bfloat16 or wider, within the bound.
A program may use at most 320 MiB of HBM per device.

v0:
```python
import math

import jax
import jax.numpy as jnp
from jax import lax
from jax.sharding import PartitionSpec as P


def standardize(v):
    centred = v - jnp.mean(v, axis=-1, keepdims=True)
    inverse = lax.rsqrt(jnp.mean(centred * centred, axis=-1, keepdims=True) + 1e-05)
    return (centred * inverse, inverse)


def norm_back(grad, normed, inverse, gain):
    scaled = grad * gain
    return inverse * (
        scaled
        - jnp.mean(scaled, axis=-1, keepdims=True)
        - normed * jnp.mean(scaled * normed, axis=-1, keepdims=True)
    )


def left_product(left, right):
    return jnp.einsum("td,te->de", left, right, preferred_element_type=jnp.float32)


def right_product(grad, weight):
    return jnp.einsum("te,de->td", grad, weight, preferred_element_type=jnp.float32)


def local(
    tokens,
    cotangent,
    segments,
    buckets,
    norm1_gain,
    norm1_bias,
    qkv_weight,
    qv_bias,
    head_scale,
    rel_table,
    out_weight,
    out_bias,
    post_gain,
    post_bias,
    norm2_gain,
    norm2_bias,
    fc1_weight,
    fc1_bias,
    inner_gain,
    inner_bias,
    fc2_weight,
    fc2_bias,
):
    f32 = jnp.float32
    bf16 = jnp.bfloat16
    rows, seq = segments.shape
    width = tokens.shape[1]
    heads = head_scale.shape[0]
    size = width // heads
    attn_full = (
        lax.all_gather(norm1_gain, ("wide", "narrow"), axis=0, tiled=True),
        lax.all_gather(norm1_bias, ("wide", "narrow"), axis=0, tiled=True),
        lax.all_gather(qkv_weight, ("wide", "narrow"), axis=0, tiled=True),
        lax.all_gather(qv_bias, ("wide", "narrow"), axis=0, tiled=True),
        lax.all_gather(rel_table, ("wide", "narrow"), axis=0, tiled=True),
        lax.all_gather(out_weight, ("wide", "narrow"), axis=0, tiled=True),
        lax.all_gather(out_bias, ("wide", "narrow"), axis=0, tiled=True),
        lax.all_gather(post_gain, ("wide", "narrow"), axis=0, tiled=True),
        lax.all_gather(post_bias, ("wide", "narrow"), axis=0, tiled=True),
    )
    ffn_full = (
        lax.all_gather(norm2_gain, ("wide", "narrow"), axis=0, tiled=True),
        lax.all_gather(norm2_bias, ("wide", "narrow"), axis=0, tiled=True),
        lax.all_gather(fc1_weight, ("wide", "narrow"), axis=0, tiled=True),
        lax.all_gather(fc1_bias, ("wide", "narrow"), axis=0, tiled=True),
        lax.all_gather(inner_gain, ("wide", "narrow"), axis=0, tiled=True),
        lax.all_gather(inner_bias, ("wide", "narrow"), axis=0, tiled=True),
        lax.all_gather(fc2_weight, ("wide", "narrow"), axis=0, tiled=True),
        lax.all_gather(fc2_bias, ("wide", "narrow"), axis=0, tiled=True),
    )
    gain_one, bias_one, w_qkv, bias_qv, table, w_attn_out, bias_attn_out, gain_post, bias_post = (
        attn_full
    )
    gain_two, bias_two, w_first, bias_first, gain_inner, bias_inner, w_second, bias_second = (
        ffn_full
    )
    scale = head_scale.astype(f32)
    inputs = tokens.astype(f32)
    hat_one, inv_one = standardize(inputs)
    h_one = (hat_one * gain_one.astype(f32) + bias_one.astype(f32)).astype(bf16)
    bias_qvf = bias_qv.astype(f32)
    shift = jnp.concatenate([bias_qvf[:width], jnp.zeros((width,), f32), bias_qvf[width:]])
    qkv = (jnp.dot(h_one, w_qkv, preferred_element_type=f32) + shift).astype(bf16)
    rel_bias = jnp.transpose(table.astype(f32)[buckets], (2, 0, 1))

    def scores_of(row):
        query = qkv[:, :width].reshape(seq, heads, size)
        key = qkv[:, width : 2 * width].reshape(seq, heads, size)
        value = qkv[:, 2 * width :].reshape(seq, heads, size)
        raw = jnp.einsum("qhd,khd->hqk", query, key, preferred_element_type=f32) * 0.125 + rel_bias
        same = segments[row][:, None] == segments[row][None, :]
        return (jnp.where(same[None], raw, -1000000000.0), query, key, value)

    row = 0
    scores, query, key, value = scores_of(row)
    top = jnp.max(scores, axis=-1, keepdims=True)
    expo = jnp.exp(scores - top)
    total = jnp.sum(expo, axis=-1, keepdims=True)
    probs = (expo / total).astype(bf16)
    lse_rows = [top + jnp.log(total)]
    attn_rows = jnp.einsum("hqk,khd->qhd", probs, value, preferred_element_type=f32)
    scaled = (attn_rows * scale[None, :, None]).reshape(-1, width).astype(bf16)
    mixed = jnp.dot(scaled, w_attn_out, preferred_element_type=f32) + bias_attn_out.astype(f32)
    hat_post, inv_post = standardize(mixed)
    first = inputs + hat_post * gain_post.astype(f32) + bias_post.astype(f32)
    hat_two, inv_two = standardize(first)
    h_two = (hat_two * gain_two.astype(f32) + bias_two.astype(f32)).astype(bf16)
    inner = jnp.dot(h_two, w_first, preferred_element_type=f32) + bias_first.astype(f32)
    gelu_out = jax.nn.gelu(inner, approximate=False)
    hat_inner, inv_inner = standardize(gelu_out)
    hidden = (hat_inner * gain_inner.astype(f32) + bias_inner.astype(f32)).astype(bf16)
    branch = jnp.dot(hidden, w_second, preferred_element_type=f32) + bias_second.astype(f32)
    output = (first + branch).astype(bf16)
    attn_back = (
        lax.all_gather(norm1_gain, ("wide", "narrow"), axis=0, tiled=True),
        lax.all_gather(norm1_bias, ("wide", "narrow"), axis=0, tiled=True),
        lax.all_gather(qkv_weight, ("wide", "narrow"), axis=0, tiled=True),
        lax.all_gather(qv_bias, ("wide", "narrow"), axis=0, tiled=True),
        lax.all_gather(rel_table, ("wide", "narrow"), axis=0, tiled=True),
        lax.all_gather(out_weight, ("wide", "narrow"), axis=0, tiled=True),
        lax.all_gather(out_bias, ("wide", "narrow"), axis=0, tiled=True),
        lax.all_gather(post_gain, ("wide", "narrow"), axis=0, tiled=True),
        lax.all_gather(post_bias, ("wide", "narrow"), axis=0, tiled=True),
    )
    ffn_back = (
        lax.all_gather(norm2_gain, ("wide", "narrow"), axis=0, tiled=True),
        lax.all_gather(norm2_bias, ("wide", "narrow"), axis=0, tiled=True),
        lax.all_gather(fc1_weight, ("wide", "narrow"), axis=0, tiled=True),
        lax.all_gather(fc1_bias, ("wide", "narrow"), axis=0, tiled=True),
        lax.all_gather(inner_gain, ("wide", "narrow"), axis=0, tiled=True),
        lax.all_gather(inner_bias, ("wide", "narrow"), axis=0, tiled=True),
        lax.all_gather(fc2_weight, ("wide", "narrow"), axis=0, tiled=True),
        lax.all_gather(fc2_bias, ("wide", "narrow"), axis=0, tiled=True),
    )
    grad_out = cotangent.astype(f32)
    g_second = left_product(hidden, cotangent)
    g_second_bias = jnp.sum(grad_out, axis=0)
    d_hidden = right_product(cotangent, ffn_back[6])
    g_inner_gain = jnp.sum(d_hidden * hat_inner, axis=0)
    g_inner_bias = jnp.sum(d_hidden, axis=0)
    d_gelu = norm_back(d_hidden, hat_inner, inv_inner, ffn_back[4].astype(f32))
    cdf = 0.5 * (1.0 + lax.erf(inner * (1.0 / math.sqrt(2.0))))
    pdf = jnp.exp(-0.5 * inner * inner) * (1.0 / math.sqrt(2.0 * math.pi))
    d_inner = (d_gelu * (cdf + inner * pdf)).astype(bf16)
    g_first_bias = jnp.sum(d_inner.astype(f32), axis=0)
    g_first = left_product(h_two, d_inner)
    d_two = right_product(d_inner, ffn_back[2])
    g_two_gain = jnp.sum(d_two * hat_two, axis=0)
    g_two_bias = jnp.sum(d_two, axis=0)
    ffn_sums = (
        lax.psum_scatter(g_two_gain, ("wide", "narrow"), scatter_dimension=0, tiled=True),
        lax.psum_scatter(g_two_bias, ("wide", "narrow"), scatter_dimension=0, tiled=True),
        lax.psum_scatter(g_first, ("wide", "narrow"), scatter_dimension=0, tiled=True),
        lax.psum_scatter(g_first_bias, ("wide", "narrow"), scatter_dimension=0, tiled=True),
        lax.psum_scatter(g_inner_gain, ("wide", "narrow"), scatter_dimension=0, tiled=True),
        lax.psum_scatter(g_inner_bias, ("wide", "narrow"), scatter_dimension=0, tiled=True),
        lax.psum_scatter(g_second, ("wide", "narrow"), scatter_dimension=0, tiled=True),
        lax.psum_scatter(g_second_bias, ("wide", "narrow"), scatter_dimension=0, tiled=True),
    )
    d_first = grad_out + norm_back(d_two, hat_two, inv_two, ffn_back[0].astype(f32))
    g_post_gain = jnp.sum(d_first * hat_post, axis=0)
    g_post_bias = jnp.sum(d_first, axis=0)
    d_mixed = norm_back(d_first, hat_post, inv_post, attn_back[7].astype(f32)).astype(bf16)
    g_attn_out_bias = jnp.sum(d_mixed.astype(f32), axis=0)
    g_attn_out = left_product(scaled, d_mixed)
    d_scaled = right_product(d_mixed, attn_back[5]).reshape(-1, heads, size)
    g_scale_local = jnp.sum(d_scaled * attn_rows, axis=(0, 2))
    scale_sum = lax.psum(g_scale_local, ("wide", "narrow"))
    d_attn = (d_scaled * scale[None, :, None]).astype(bf16)
    row = 0
    scores, query, key, value = scores_of(row)
    probs = jnp.exp(scores - lse_rows[row])
    d_value = jnp.einsum("hqk,qhd->khd", probs.astype(bf16), d_attn, preferred_element_type=f32)
    d_probs = jnp.einsum("qhd,khd->hqk", d_attn, value, preferred_element_type=f32)
    delta = jnp.sum(probs * d_probs, axis=-1, keepdims=True)
    d_scores = (probs * (d_probs - delta)).astype(bf16)
    d_query = jnp.einsum("hqk,khd->qhd", d_scores, key, preferred_element_type=f32) * 0.125
    d_key = jnp.einsum("hqk,qhd->khd", d_scores, query, preferred_element_type=f32) * 0.125
    bias_grad = d_scores.astype(f32)
    dqkv_rows = jnp.concatenate(
        [d_query.reshape(seq, width), d_key.reshape(seq, width), d_value.reshape(seq, width)],
        axis=1,
    ).astype(bf16)
    g_table = jax.ops.segment_sum(
        jnp.transpose(bias_grad, (1, 2, 0)).reshape(seq * seq, heads),
        buckets.reshape(-1),
        num_segments=attn_back[4].shape[0],
    )
    qkv_sum = jnp.sum(dqkv_rows.astype(f32), axis=0)
    g_qv = jnp.concatenate([qkv_sum[:width], qkv_sum[2 * width :]])
    g_qkv = left_product(h_one, dqkv_rows)
    d_one = right_product(dqkv_rows, attn_back[2])
    g_one_gain = jnp.sum(d_one * hat_one, axis=0)
    g_one_bias = jnp.sum(d_one, axis=0)
    attn_sums = (
        lax.psum_scatter(g_one_gain, ("wide", "narrow"), scatter_dimension=0, tiled=True),
        lax.psum_scatter(g_one_bias, ("wide", "narrow"), scatter_dimension=0, tiled=True),
        lax.psum_scatter(g_qkv, ("wide", "narrow"), scatter_dimension=0, tiled=True),
        lax.psum_scatter(g_qv, ("wide", "narrow"), scatter_dimension=0, tiled=True),
        lax.psum_scatter(g_table, ("wide", "narrow"), scatter_dimension=0, tiled=True),
        lax.psum_scatter(g_attn_out, ("wide", "narrow"), scatter_dimension=0, tiled=True),
        lax.psum_scatter(g_attn_out_bias, ("wide", "narrow"), scatter_dimension=0, tiled=True),
        lax.psum_scatter(g_post_gain, ("wide", "narrow"), scatter_dimension=0, tiled=True),
        lax.psum_scatter(g_post_bias, ("wide", "narrow"), scatter_dimension=0, tiled=True),
    )
    grad_tokens = (d_first + norm_back(d_one, hat_one, inv_one, attn_back[0].astype(f32))).astype(
        bf16
    )
    return (
        output,
        grad_tokens,
        attn_sums[0],
        attn_sums[1],
        attn_sums[2],
        attn_sums[3],
        scale_sum,
        attn_sums[4],
        attn_sums[5],
        attn_sums[6],
        attn_sums[7],
        attn_sums[8],
        ffn_sums[0],
        ffn_sums[1],
        ffn_sums[2],
        ffn_sums[3],
        ffn_sums[4],
        ffn_sums[5],
        ffn_sums[6],
        ffn_sums[7],
    )


def solution(mesh):
    return jax.shard_map(
        local,
        mesh=mesh,
        in_specs=(
            P(("wide", "narrow"), None),
            P(("wide", "narrow"), None),
            P(("wide", "narrow"), None),
            P(),
            P(("wide", "narrow")),
            P(("wide", "narrow")),
            P(("wide", "narrow"), None),
            P(("wide", "narrow")),
            P(),
            P(("wide", "narrow"), None),
            P(("wide", "narrow"), None),
            P(("wide", "narrow")),
            P(("wide", "narrow")),
            P(("wide", "narrow")),
            P(("wide", "narrow")),
            P(("wide", "narrow")),
            P(("wide", "narrow"), None),
            P(("wide", "narrow")),
            P(("wide", "narrow")),
            P(("wide", "narrow")),
            P(("wide", "narrow"), None),
            P(("wide", "narrow")),
        ),
        out_specs=(
            P(("wide", "narrow"), None),
            P(("wide", "narrow"), None),
            P(("wide", "narrow")),
            P(("wide", "narrow")),
            P(("wide", "narrow"), None),
            P(("wide", "narrow")),
            P(),
            P(("wide", "narrow"), None),
            P(("wide", "narrow"), None),
            P(("wide", "narrow")),
            P(("wide", "narrow")),
            P(("wide", "narrow")),
            P(("wide", "narrow")),
            P(("wide", "narrow")),
            P(("wide", "narrow"), None),
            P(("wide", "narrow")),
            P(("wide", "narrow")),
            P(("wide", "narrow")),
            P(("wide", "narrow"), None),
            P(("wide", "narrow")),
        ),
        check_vma=False,
    )
```

profile of v0, /device:TPU:0, one launch (start us, length us, event | category | flops | bytes accessed | tf_op | source)
XLA Modules:
  0.0 3289.9 jit_solution(7633699013007605415)
XLA Ops:
  10.1 0.8 dynamic-update-slice.1
  10.9 0.8 dynamic-update-slice
  15.9 0.8 dynamic-update-slice.8
  16.8 0.8 dynamic-update-slice.10
  17.6 0.8 dynamic-update-slice.9
  18.5 0.8 dynamic-update-slice.11
  19.3 0.8 dynamic-update-slice.2
  20.1 43.4 %all-reduce.26 = (bf16[1536]{0:T(1024)(128)(2,1)S(1)}, bf16[768]{0:T(1024)(128)(2,1)S(1)}, bf16[768]{0:T(1024)(128)(2,1)S(1)}, bf16[768]{0:T(1024)(128)(2,1)S(1)...) all-reduce(bf16[1536]{0:T(1024)(128)(2,1)S(1)} %dynamic-update-slic, ...), channel_id=1, replica_groups=mesh['wide'=8,'narrow'=4] {'wide','narrow'}, use_global_device_ids=true, to_apply=%add.2 | all-reduce | flops 16896 | bytes 67584
  65.3 1.2 convert_element_type.117
  68.3 1.3 convert_reduce_fusion.2
  69.6 1.5 fusion.43
  71.7 41.3 %all_gather.63 = bf16[256,12]{1,0:T(8,128)(2,1)S(1)} all-gather(bf16[8,12]{1,0:T(8,128)(2,1)} %param.31), channel_id=1, replica_groups=mesh['wide'=8,'narrow'=4] {'wide','narrow'}, dimensions={0}, use_global_device_ids=true | all-gather | bytes 6336 | tf_op jit(solution)/shard_map/all_gather | solution.py:67
  113.0 1.4 fusion.50
  114.8 860.1 %gather_fusion = f32[262144,12]{1,0:T(8,128)} fusion(f32[256,12]{1,0:T(8,128)S(1)} %convert_element_type.115, s32[262144]{0:T(1024)S(1)} %broadcast_clamp_fusion), kind=kCustom, calls=%fused_computation | custom fusion | bytes 26214400 | tf_op jit(solution)/shard_map/gather | solution.py:96
  975.1 73.6 %copy.70 = f32[512,512,12]{0,1,2:T(8,128)} copy(f32[512,512,12]{2,1,0:T(8,128)} %bitcast.4) | data formatting | bytes 25165824 | tf_op jit(solution)/shard_map/gather | solution.py:96
  1050.2 1.3 copy.90
  1051.5 4.2 fusion.28
  1056.4 12.9 fusion.65
  1069.3 6.4 fusion.6
  1076.0 8.3 fusion.45
  1084.4 2.4 fusion.70
  1089.0 19.8 fusion.61
  1108.7 2.7 copy-done
  1112.2 8.6 multiply_reduce_fusion.1
  1120.9 9.4 convert_reduce_fusion
  1130.4 7.1 multiply_reduce_fusion.5
  1137.5 2.3 multiply_reduce_fusion.6
  1139.8 1.1 convert_reduce_fusion.4
  1141.8 2.1 fusion.47
  1143.9 6.0 multiply_reduce_fusion
  1149.9 7.1 multiply_convert_fusion
  1157.0 2.0 multiply_convert_fusion.1
  1159.1 1.1 multiply_convert_fusion.2
  1162.1 1.2 slice-done.5
  1163.3 15.5 fusion.18
  1178.8 62.2 %copy.87 = f32[512,512,12]{2,1,0:T(8,128)} copy(f32[512,512,12]{0,1,2:T(8,128)} %fusion.18) | data formatting | bytes 25165824 | tf_op jit(solution)/shard_map/reshape | solution.py:197
  1241.5 1387.0 %scatter_custom_fusion = f32[256,12]{1,0:T(8,128)} fusion(s32[262144]{0:T(1024)} %bitcast.106, f32[262144,12]{1,0:T(8,128)} %bitcast.19, f32[]{:T(128)} %constant.40.clone.1), kind=kCustom, calls=%fused_computation.107 | custom fusion | flops 3145728 | bytes 12800 | tf_op jit(solution)/shard_map/scatter-add | solution.py:196
  2628.5 6.6 fusion.42
  2635.2 3.6 fusion.72
  2639.1 6.6 fusion.54
  2646.4 7.2 fusion.58
  2653.7 1.1 copy-done.21
  2654.7 8.2 fusion.73
  2664.3 3.2 fusion.41
  2667.6 5.8 add_convert_fusion.1
  2673.4 94.2 %all-reduce.29.cloned.1.call-done = (f32[768]{0:T(1024)}, f32[768]{0:T(1024)}, f32[1536]{0:T(1024)}, f32[12]{0:T(128)}, f32[256,12]{1,0:T(8,128)}, /*index=5*/f3...) async-done(((f32[768]{0:T(1024)}, f32[768]{0:T(1024)}, ...) | async-done | bytes 79936
  2767.6 1.3 dynamic-slice
  2768.9 1.3 dynamic-slice.1
  2770.2 1.3 dynamic-slice.4
  2771.4 1.3 dynamic-slice.5
  2772.7 1.3 dynamic-slice.6
  2773.9 1.3 dynamic-slice.7
  2775.2 1.3 dynamic-slice.8
  2776.5 1.3 dynamic-slice.9
  2777.7 1.3 dynamic-slice.10
  2779.0 1.3 dynamic-slice.11
  2780.3 1.3 dynamic-slice.12
  2781.6 1.3 dynamic-slice.2
  2782.8 1.3 constant_dynamic-slice_fusion
  2784.1 90.0 %reduce-scatter.7.cloned.1.call-done = f32[24,768]{1,0:T(8,128)} async-done(((f32[768,768]{1,0:T(8,128)}), f32[24,768]{1,0:T(8,128)}) %reduce-scatter.7.cloned.1.call-update) | async-done | bytes 73744 | tf_op jit(solution)/shard_map/reduce_scatter | solution.py:213
  2874.1 124.8 %reduce-scatter.5.cloned.1.call-done = f32[24,2304]{1,0:T(8,128)} async-done(((f32[768,2304]{1,0:T(8,128)}), f32[24,2304]{1,0:T(8,128)}) %reduce-scatter.5.cloned.1.call-update) | async-done | bytes 221200 | tf_op jit(solution)/shard_map/reduce_scatter | solution.py:210
  2998.9 141.6 %reduce-scatter.9.cloned.1.call-done = f32[24,3072]{1,0:T(8,128)} async-done(((f32[768,3072]{1,0:T(8,128)}), f32[24,3072]{1,0:T(8,128)}) %reduce-scatter.9.cloned.1.call-update) | async-done | bytes 294928 | tf_op jit(solution)/shard_map/reduce_scatter | solution.py:165
  3140.5 141.6 %reduce-scatter.11.cloned.1.call-done = f32[96,768]{1,0:T(8,128)} async-done(((f32[3072,768]{1,0:T(8,128)}), f32[96,768]{1,0:T(8,128)}) %reduce-scatter.11.cloned.1.call-update) | async-done | bytes 294928 | tf_op jit(solution)/shard_map/reduce_scatter | solution.py:169
  3282.1 1.1 copy.117
  (201 shorter events, 22.8 us)
Async XLA Ops:
  7.2 1044.3 %all-gather.5.cloned.1.call-start = ((), (), s32[]{:S(2)}) async-start(), calls=%async_computation.4 | async-start | bytes 3649536 | tf_op jit(solution)/shard_map/all_gather | solution.py:65
  7.9 1076.4 %all-gather.7.cloned.1.call-start = ((), (), s32[]{:S(2)}) async-start(), calls=%async_computation.5 | async-start | bytes 1216512 | tf_op jit(solution)/shard_map/all_gather | solution.py:68
  8.7 1080.3 %all-gather.9.cloned.1.call-start = ((), (), s32[]{:S(2)}) async-start(), calls=%async_computation.6 | async-start | bytes 4866048 | tf_op jit(solution)/shard_map/all_gather | solution.py:76
  9.4 1102.8 %all-gather.11.cloned.1.call-start = ((), (), s32[]{:S(2)}) async-start(), calls=%async_computation.7 | async-start | bytes 4866048 | tf_op jit(solution)/shard_map/all_gather | solution.py:80
  10.0 2757.7 %all-reduce.29.cloned.1.call-start = ((), (), s32[]{:S(2)}) async-start(), calls=%async_computation.12 | async-start | bytes 418816
  69.6 43.4 %copy-start.24 = (f32[512]{0:T(512)}, f32[512]{0:T(512)S(1)}, u32[]{:S(2)}) copy-start(f32[512]{0:T(512)S(1)} %broadcast_multiply_fusion.11) | copy-start | bytes 6148
  974.9 73.7 %copy-start.35 = (s32[1,512]{1,0:T(1,128)S(1)}, s32[1,512]{1,0:T(1,128)}, u32[]{:S(2)}) copy-start(s32[1,512]{1,0:T(1,128)} %param.24) | copy-start | bytes 6148
  974.9 74.0 %copy-start.41 = (bf16[3072]{0:T(1024)(128)(2,1)S(1)}, bf16[3072]{0:T(1024)(128)(2,1)}, u32[]{:S(2)}) copy-start(bf16[3072]{0:T(1024)(128)(2,1)} %get-tuple-element.58) | copy-start | bytes 18436
  975.0 74.0 %copy-start.50 = (bf16[768]{0:T(1024)(128)(2,1)S(1)}, bf16[768]{0:T(1024)(128)(2,1)}, u32[]{:S(2)}) copy-start(bf16[768]{0:T(1024)(128)(2,1)} %get-tuple-element.56) | copy-start | bytes 4612
  975.0 74.6 %copy-start.49 = (bf16[768]{0:T(1024)(128)(2,1)S(1)}, bf16[768]{0:T(1024)(128)(2,1)}, u32[]{:S(2)}) copy-start(bf16[768]{0:T(1024)(128)(2,1)} %get-tuple-element.57) | copy-start | bytes 4612
  975.0 75.2 %copy-start.40 = (bf16[3072]{0:T(1024)(128)(2,1)S(1)}, bf16[3072]{0:T(1024)(128)(2,1)}, u32[]{:S(2)}) copy-start(bf16[3072]{0:T(1024)(128)(2,1)} %get-tuple-element.60) | copy-start | bytes 18436
  975.0 75.2 %copy-start.39 = (bf16[3072]{0:T(1024)(128)(2,1)S(1)}, bf16[3072]{0:T(1024)(128)(2,1)}, u32[]{:S(2)}) copy-start(bf16[3072]{0:T(1024)(128)(2,1)} %get-tuple-element.59) | copy-start | bytes 18436
  975.0 75.2 %copy-start.11 = (s32[512,512]{1,0:T(8,128)S(1)}, s32[512,512]{1,0:T(8,128)}, u32[]{:S(2)}) copy-start(s32[512,512]{1,0:T(8,128)} %param.25) | copy-start | bytes 3145732
  975.0 76.4 %copy-start.30 = (f32[768]{0:T(1024)S(1)}, f32[768]{0:T(1024)}, u32[]{:S(2)}) copy-start(f32[768]{0:T(1024)} %get-tuple-element.80) | copy-start | bytes 9220
  975.0 76.4 %copy-start.31 = (f32[768]{0:T(1024)S(1)}, f32[768]{0:T(1024)}, u32[]{:S(2)}) copy-start(f32[768]{0:T(1024)} %get-tuple-element.81) | copy-start | bytes 9220
  975.0 76.5 %copy-start.4 = (bf16[512,768]{1,0:T(8,128)(2,1)S(1)}, bf16[512,768]{1,0:T(8,128)(2,1)}, u32[]{:S(2)}) copy-start(bf16[512,768]{1,0:T(8,128)(2,1)} %param.22) | copy-start | bytes 2359300
  975.0 76.5 %copy-start.25 = (f32[512]{0:T(512)S(1)}, f32[512]{0:T(512)}, u32[]{:S(2)}) copy-start(f32[512]{0:T(512)} %copy-done.24) | copy-start | bytes 6148
  975.0 76.5 %copy-start.32 = (f32[768]{0:T(1024)S(1)}, f32[768]{0:T(1024)}, u32[]{:S(2)}) copy-start(f32[768]{0:T(1024)} %convert_element_type.110) | copy-start | bytes 9220
  975.1 76.5 %copy-start.36 = (f32[512]{0:T(512)S(1)}, f32[512]{0:T(512)}, u32[]{:S(2)}) copy-start(f32[512]{0:T(512)} %add_rsqrt_fusion.3) | copy-start | bytes 6148
  975.1 76.5 %copy-start.42 = (f32[768]{0:T(1024)S(1)}, f32[768]{0:T(1024)}, u32[]{:S(2)}) copy-start(f32[768]{0:T(1024)} %convert_element_type.111) | copy-start | bytes 9220
  1056.1 13.2 copy-start.9
  1056.4 12.9 copy-start.7
  1069.3 6.7 copy-start.46
  1076.0 8.3 copy-start.12
  1076.0 8.4 copy-start.45
  1084.3 2.8 copy-start.22
  1084.3 2.8 copy-start.23
  1084.3 2.9 copy-start.34
  1084.3 2.8 copy-start.5
  1108.7 2.7 copy-start
  1112.2 8.6 copy-start.1
  1120.9 9.5 copy-start.28
  1120.9 9.5 copy-start.29
  1120.9 9.5 copy-start.38
  1130.3 7.1 copy-start.16
  1130.3 7.1 copy-start.20
  1130.3 11.4 slice-start
  1130.4 11.4 slice-start.1
  1137.5 3.4 copy-start.51
  1137.5 4.2 slice-start.2
  1139.8 1.9 copy-start.2
  1139.8 2.0 copy-start.47
  1140.9 3.0 copy-start.17
  1141.8 2.1 copy-start.13
  1143.9 16.3 copy-start.14
  1149.9 7.1 copy-start.10
  1157.0 2.0 copy-start.8
  1157.0 4.5 slice-start.3
  1159.0 1.2 copy-start.18
  1159.0 1.7 copy-start.19
  1159.0 3.0 slice-start.4
  1159.0 4.2 slice-start.5
  1178.7 1449.8 %copy-start.6 = (bf16[512,768]{1,0:T(8,128)(2,1)S(1)}, bf16[512,768]{1,0:T(8,128)(2,1)}, u32[]{:S(2)}) copy-start(bf16[512,768]{1,0:T(8,128)(2,1)} %param.22) | copy-start | bytes 2359300
  1178.7 1449.8 %copy-start.26 = (f32[512]{0:T(512)S(1)}, f32[512]{0:T(512)}, u32[]{:S(2)}) copy-start(f32[512]{0:T(512)} %copy-done.24) | copy-start | bytes 6148
  1178.8 1449.8 %copy-start.33 = (f32[768]{0:T(1024)S(1)}, f32[768]{0:T(1024)}, u32[]{:S(2)}) copy-start(f32[768]{0:T(1024)} %convert_element_type.110) | copy-start | bytes 9220
  1178.8 1449.8 %copy-start.37 = (f32[512]{0:T(512)S(1)}, f32[512]{0:T(512)}, u32[]{:S(2)}) copy-start(f32[512]{0:T(512)} %add_rsqrt_fusion.3) | copy-start | bytes 6148
  2635.2 3.9 copy-start.43
  2635.2 238.9 %reduce-scatter.7.cloned.1.call-start = ((), (), s32[]{:S(2)}) async-start(), calls=%async_computation.9 | async-start | bytes 2433024 | tf_op jit(solution)/shard_map/reduce_scatter | solution.py:213
  2638.8 360.1 %reduce-scatter.5.cloned.1.call-start = ((), (), s32[]{:S(2)}) async-start(), calls=%async_computation.8 | async-start | bytes 7299072 | tf_op jit(solution)/shard_map/reduce_scatter | solution.py:210
  2645.7 494.7 %reduce-scatter.9.cloned.1.call-start = ((), (), s32[]{:S(2)}) async-start(), calls=%async_computation.10 | async-start | bytes 9732096 | tf_op jit(solution)/shard_map/reduce_scatter | solution.py:165
  2653.6 1.1 copy-start.21
  2653.6 628.4 %reduce-scatter.11.cloned.1.call-start = ((), (), s32[]{:S(2)}) async-start(), calls=%async_computation.11 | async-start | bytes 9732096 | tf_op jit(solution)/shard_map/reduce_scatter | solution.py:169
  2662.9 1.4 copy-start.3
  2663.6 4.0 copy-start.15
  (3 other events, 1.9 us)
Sparse Core Ops, SparseCore 0:
  10.9 63.3 all-gather.4
  77.2 52.6 all-gather.6
  132.9 62.4 all-gather.8
  198.1 61.8 all-gather.10
  2635.3 132.2 all-reduce.28
  2773.4 100.6 reduce-scatter.6
  2880.3 118.5 reduce-scatter.4
  3005.4 135.0 reduce-scatter.8
  3146.9 135.0 reduce-scatter.10
where the time goes:
time: 3300 us; the launch traced here: 3290 us
  other arithmetic  1450 us (44%)
  local copies, waits for them, and re-layouts  1030 us (31%)
  waiting for transfers between devices  595 us (18%)
  matrix products  113 us (3%)
  blocking collectives  84.7 us (3%)
    scatter-add x1, other arithmetic, local(): jax.ops.segment_sum(jnp.transpose(bias_grad, (1, 2, 0)).reshape(seq * seq...  1390 us
    gather x2, local copies, waits for them, and re-layouts, local(): rel_bias = jnp.transpose(table.astype(f32)[buckets], (2, 0, 1))  934 us
    reduce_scatter x1, waiting for transfers between devices, local(): lax.psum_scatter(g_second, ('wide', 'narrow'), scatter_dimension=0, tiled...  142 us
    reduce_scatter x1, waiting for transfers between devices, local(): lax.psum_scatter(g_first, ('wide', 'narrow'), scatter_dimension=0, tiled=...  142 us
    reduce_scatter x1, waiting for transfers between devices, local(): lax.psum_scatter(g_qkv, ('wide', 'narrow'), scatter_dimension=0, tiled=True)  125 us
    unnamed x10, waiting for transfers between devices  96.9 us
    reduce_scatter x1, waiting for transfers between devices, local(): lax.psum_scatter(g_attn_out, ('wide', 'narrow'), scatter_dimension=0, til...  90 us
  transfers between devices with their start and end apart: 9, of which 5 were waited for; matrix products, arithmetic and copies ran while one was open for 32% of the time, Pallas kernels for 0%

commit v1 on v0

v1 whole, which is shorter than its diff:
```python
import functools
import math

import jax, jax.numpy as jnp
from jax import lax
from jax.experimental import pallas as pl
from jax.experimental.pallas import tpu as pltpu
from jax.sharding import PartitionSpec as P

f32 = jnp.float32
bf16 = jnp.bfloat16
NT = (((1,), (1,)), ((), ()))
TN = (((0,), (0,)), ((), ()))


def dot(a, b, dims=(((1,), (0,)), ((), ()))):
    return lax.dot_general(a, b, dims, preferred_element_type=f32)


def lookup(row, index):
    shape = index.shape
    low = jnp.broadcast_to(row[:, :128], shape)
    high = jnp.broadcast_to(row[:, 128:], shape)
    inner = index & 127
    return jnp.where(
        index < 128,
        jnp.take_along_axis(low, inner, axis=1),
        jnp.take_along_axis(high, inner, axis=1),
    )


def forward_kernel(q_ref, k_ref, v_ref, table_ref, buckets_ref, segc_ref, segr_ref,
                   attn_ref, p_ref):
    seq = q_ref.shape[0]
    pair = pl.program_id(0)
    even = lax.broadcasted_iota(jnp.int32, (1, 128), 1) < 64
    rows = 128
    for half in range(2):
        mine = even if half == 0 else jnp.logical_not(even)
        row = table_ref[0, half : half + 1, :]
        k = k_ref[...]
        v = v_ref[...]

        def body(step, carry):
            at = pl.ds(pl.multiple_of(step * rows, rows), rows)
            q = jnp.where(mine, q_ref[at, :], jnp.zeros((), bf16))
            raw = dot(q, k, NT) * 0.125
            bias = jnp.concatenate(
                [lookup(row, buckets_ref[at, pl.ds(128 * j, 128)]) for j in range(seq // 128)], axis=1
            )
            same = segc_ref[at, :] == segr_ref[...]
            scores = jnp.where(same, raw + bias, -1e9)
            top = jnp.max(scores, axis=1, keepdims=True)
            expo = jnp.exp(scores - top)
            total = jnp.sum(expo, axis=1, keepdims=True)
            probs = (expo * (1.0 / total)).astype(bf16)
            p_ref[half, at, :] = probs
            out = dot(probs, v)
            if half == 0:
                attn_ref[at, :] = out
            else:
                attn_ref[at, :] = jnp.where(even, attn_ref[at, :], out)
            return carry

        lax.fori_loop(0, seq // rows, body, 0)


def attention_forward(qkv, table_t, buckets, segments):
    seq, width = qkv.shape[0], qkv.shape[1] // 3
    pairs = width // 128
    nb = table_t.shape[2]
    return pl.pallas_call(
        forward_kernel,
        grid=(pairs,),
        in_specs=[
            pl.BlockSpec((seq, 128), lambda i: (0, i)),
            pl.BlockSpec((seq, 128), lambda i: (0, pairs + i)),
            pl.BlockSpec((seq, 128), lambda i: (0, 2 * pairs + i)),
            pl.BlockSpec((1, 2, nb), lambda i: (i, 0, 0)),
            pl.BlockSpec((seq, seq), lambda i: (0, 0)),
            pl.BlockSpec((seq, 1), lambda i: (0, 0)),
            pl.BlockSpec((1, seq), lambda i: (0, 0)),
        ],
        out_specs=[
            pl.BlockSpec((seq, 128), lambda i: (0, i)),
            pl.BlockSpec((2, seq, seq), lambda i: (i, 0, 0)),
        ],
        out_shape=[
            jax.ShapeDtypeStruct((seq, width), f32),
            jax.ShapeDtypeStruct((2 * pairs, seq, seq), bf16),
        ],
        name="attention_forward",
    )(qkv, qkv, qkv, table_t, buckets, segments.reshape(seq, 1), segments.reshape(1, seq))


HIGH = 4


def backward_kernel(q_ref, k_ref, v_ref, do_ref, attn_ref, p_ref, buckets_ref,
                    dq_ref, dk_ref, dv_ref, hist_ref, ds_ref, dst_ref, acc_ref):
    seq = q_ref.shape[0]
    heads = p_ref.shape[0] * pl.num_programs(0)
    pair = pl.program_id(0)
    even = lax.broadcasted_iota(jnp.int32, (1, 128), 1) < 64
    rows = 128
    chunks = seq // 128
    for half in range(2):
        mine = even if half == 0 else jnp.logical_not(even)
        k = k_ref[...]
        v = v_ref[...]
        head = pair * 2 + half

        def body(step, carry):
            at = pl.ds(pl.multiple_of(step * rows, rows), rows)
            do = jnp.where(mine, do_ref[at, :], jnp.zeros((), bf16))
            probs = p_ref[half, at, :]
            delta = jnp.sum(do.astype(f32) * attn_ref[at, :], axis=1, keepdims=True)
            ds = probs.astype(f32) * (dot(do, v, NT) - delta)
            for j in range(chunks):
                ds_ref[j, pl.ds(step * rows * 16 + head, rows, stride=16), :] = ds[:, 128 * j : 128 * j + 128]
            ds = ds.astype(bf16)
            dst_ref[at, :] = ds
            dq = dot(ds, k) * 0.125
            if half == 0:
                dq_ref[at, :] = dq.astype(bf16)
            else:
                dq_ref[at, :] = jnp.where(even, dq_ref[at, :], dq.astype(bf16))
            return carry

        lax.fori_loop(0, seq // rows, body, 0)
        dk = (dot(dst_ref[...], q_ref[...], TN) * 0.125).astype(bf16)
        dv = dot(p_ref[half], do_ref[...], TN).astype(bf16)
        if half == 0:
            dk_ref[...] = dk
            dv_ref[...] = dv
        else:
            dk_ref[...] = jnp.where(even, dk_ref[...], dk)
            dv_ref[...] = jnp.where(even, dv_ref[...], dv)

    @pl.when(pair == pl.num_programs(0) - 1)
    def _():
        acc_ref[...] = jnp.zeros_like(acc_ref)
        group = 8
        low = acc_ref.shape[1]

        def body(step, carry):
            base = pl.multiple_of(step * group, group)
            ids = buckets_ref[pl.ds(base, group), :]
            left, right = [], []
            for r in range(group):
                at = pl.ds(pl.multiple_of((base + r) * 16, 16), 16)
                d = jnp.concatenate([ds_ref[j, at, :] for j in range(chunks)], axis=1)
                idr = ids[r : r + 1, :]
                top = idr // low
                left.append(jnp.concatenate(
                    [jnp.where(top == b, d, 0.0) for b in range(HIGH)], axis=0).astype(bf16))
                which = lax.broadcasted_iota(jnp.int32, (low, seq), 0)
                right.append(jnp.where(which == (idr & (low - 1)), 1.0, 0.0).astype(bf16))
            acc_ref[...] += dot(jnp.concatenate(left, axis=1), jnp.concatenate(right, axis=1), NT)
            return carry

        lax.fori_loop(0, seq // group, body, 0)
        hist_ref[...] = acc_ref[...]


def attention_backward(qkv, d_attn, attn, p, buckets, nb):
    seq, width = d_attn.shape
    pairs = width // 128
    low = nb // HIGH
    narrow = lambda first: pl.BlockSpec((seq, 128), lambda i: (0, first + i))
    return pl.pallas_call(
        backward_kernel,
        grid=(pairs,),
        in_specs=[
            narrow(0), narrow(pairs), narrow(2 * pairs), narrow(0), narrow(0),
            pl.BlockSpec((2, seq, seq), lambda i: (i, 0, 0)),
            pl.BlockSpec((seq, seq), lambda i: (0, 0)),
        ],
        out_specs=[narrow(0), narrow(0), narrow(0), pl.BlockSpec((HIGH * 16, low), lambda i: (0, 0))],
        out_shape=[jax.ShapeDtypeStruct((seq, width), bf16)] * 3
        + [jax.ShapeDtypeStruct((HIGH * 16, low), f32)],
        scratch_shapes=[
            pltpu.VMEM((seq // 128, seq * 16, 128), f32),
            pltpu.VMEM((seq, seq), bf16),
            pltpu.VMEM((HIGH * 16, low), f32),
        ],
        name="attention_backward",
    )(qkv, qkv, qkv, d_attn, attn, p, buckets)


def table_gradient(hist, heads):
    high, low = HIGH, hist.shape[1]
    return hist.reshape(high, 16, low)[:, :heads].transpose(0, 2, 1).reshape(high * low, heads)

AXES = ("wide", "narrow")


def standardize(v):
    centred = v - jnp.mean(v, axis=-1, keepdims=True)
    inverse = lax.rsqrt(jnp.mean(centred * centred, axis=-1, keepdims=True) + 1e-05)
    return centred * inverse, inverse


def norm_back(grad, normed, inverse, gain):
    scaled = grad * gain
    return inverse * (
        scaled
        - jnp.mean(scaled, axis=-1, keepdims=True)
        - normed * jnp.mean(scaled * normed, axis=-1, keepdims=True)
    )


def pack(vectors, devices):
    return jnp.concatenate([v.reshape(devices, -1) for v in vectors], axis=1)


def unpack(packed, sizes):
    out, at = [], 0
    for size in sizes:
        out.append(packed[:, at : at + size].reshape(-1))
        at += size
    return out


def gather(x):
    return lax.all_gather(x, AXES, axis=0, tiled=True)


def scatter(x):
    return lax.psum_scatter(x, AXES, scatter_dimension=0, tiled=True)


def local(devices, tokens, cotangent, segments, buckets, norm1_gain, norm1_bias, qkv_weight, qv_bias,
          head_scale, rel_table, out_weight, out_bias, post_gain, post_bias, norm2_gain, norm2_bias,
          fc1_weight, fc1_bias, inner_gain, inner_bias, fc2_weight, fc2_bias):
    seq, width = tokens.shape
    heads = head_scale.shape[0]
    size = width // heads
    small = (norm1_gain, norm1_bias, out_bias, post_gain, post_bias, norm2_gain, norm2_bias, fc2_bias,
             qv_bias, fc1_bias, inner_gain, inner_bias, rel_table.reshape(-1))
    sizes = [v.shape[0] for v in small]
    nb = rel_table.shape[0] * devices
    packed = gather(jnp.concatenate(small)[None, :])
    w_qkv = gather(qkv_weight)
    w_out = gather(out_weight)
    w_first = gather(fc1_weight)
    w_second = gather(fc2_weight)
    (gain_one, bias_one, bias_out, gain_post, bias_post, gain_two, bias_two, bias_second,
     bias_qv, bias_first, gain_inner, bias_inner, table) = [v.astype(f32) for v in unpack(packed, sizes)]
    table_t = table.reshape(nb, heads).T.reshape(heads // 2, 2, nb)
    scale = jnp.repeat(head_scale.astype(f32), size)[None, :]

    inputs = tokens.astype(f32)
    hat_one, inv_one = standardize(inputs)
    h_one = (hat_one * gain_one + bias_one).astype(bf16)
    shift = jnp.concatenate([bias_qv[:width], jnp.zeros((width,), f32), bias_qv[width:]])
    qkv = (dot(h_one, w_qkv) + shift).astype(bf16)
    attn, probs = attention_forward(qkv, table_t, buckets, segments)
    scaled = (attn * scale).astype(bf16)
    mixed = dot(scaled, w_out) + bias_out
    hat_post, inv_post = standardize(mixed)
    first = inputs + hat_post * gain_post + bias_post
    hat_two, inv_two = standardize(first)
    h_two = (hat_two * gain_two + bias_two).astype(bf16)
    inner = dot(h_two, w_first) + bias_first
    cdf = 0.5 * (1.0 + lax.erf(inner * (1.0 / math.sqrt(2.0))))
    hat_inner, inv_inner = standardize(inner * cdf)
    hidden = (hat_inner * gain_inner + bias_inner).astype(bf16)
    output = (first + (dot(hidden, w_second) + bias_second)).astype(bf16)

    grad_out = cotangent.astype(f32)
    g_second = scatter(dot(hidden, cotangent, TN))
    g_second_bias = jnp.sum(grad_out, axis=0)
    d_hidden = dot(cotangent, w_second, NT)
    g_inner_gain = jnp.sum(d_hidden * hat_inner, axis=0)
    g_inner_bias = jnp.sum(d_hidden, axis=0)
    d_gelu = norm_back(d_hidden, hat_inner, inv_inner, gain_inner)
    pdf = jnp.exp(-0.5 * inner * inner) * (1.0 / math.sqrt(2.0 * math.pi))
    d_inner = (d_gelu * (cdf + inner * pdf)).astype(bf16)
    g_first_bias = jnp.sum(d_inner.astype(f32), axis=0)
    g_first = scatter(dot(h_two, d_inner, TN))
    d_two = dot(d_inner, w_first, NT)
    g_two_gain = jnp.sum(d_two * hat_two, axis=0)
    g_two_bias = jnp.sum(d_two, axis=0)
    d_first = grad_out + norm_back(d_two, hat_two, inv_two, gain_two)
    g_post_gain = jnp.sum(d_first * hat_post, axis=0)
    g_post_bias = jnp.sum(d_first, axis=0)
    d_mixed = norm_back(d_first, hat_post, inv_post, gain_post).astype(bf16)
    g_out_bias = jnp.sum(d_mixed.astype(f32), axis=0)
    g_out = scatter(dot(scaled, d_mixed, TN))
    d_scaled = dot(d_mixed, w_out, NT)
    g_scale = jnp.sum(jnp.sum(d_scaled * attn, axis=0).reshape(heads, size), axis=1)
    d_attn = (d_scaled * scale).astype(bf16)
    dq, dk, dv, hist = attention_backward(qkv, d_attn, attn, probs, buckets, nb)
    g_table = table_gradient(hist, heads)
    dqkv = jnp.concatenate([dq, dk, dv], axis=1)
    g_qv = jnp.concatenate([jnp.sum(dq.astype(f32), axis=0), jnp.sum(dv.astype(f32), axis=0)])
    g_qkv = scatter(dot(h_one, dqkv, TN))
    d_one = dot(dqkv, w_qkv, NT)
    g_one_gain = jnp.sum(d_one * hat_one, axis=0)
    g_one_bias = jnp.sum(d_one, axis=0)
    grad_tokens = (d_first + norm_back(d_one, hat_one, inv_one, gain_one)).astype(bf16)

    grads = (g_one_gain, g_one_bias, g_out_bias, g_post_gain, g_post_bias, g_two_gain, g_two_bias,
             g_second_bias, g_qv, g_first_bias, g_inner_gain, g_inner_bias, g_table.reshape(-1))
    summed = scatter(pack(grads, devices))
    g_scale = lax.psum(g_scale, AXES)
    (g_one_gain, g_one_bias, g_out_bias, g_post_gain, g_post_bias, g_two_gain, g_two_bias,
     g_second_bias, g_qv, g_first_bias, g_inner_gain, g_inner_bias, g_table) = unpack(summed, sizes)
    g_table = g_table.reshape(rel_table.shape)
    return (output, grad_tokens, g_one_gain, g_one_bias, g_qkv, g_qv, g_scale, g_table, g_out, g_out_bias,
            g_post_gain, g_post_bias, g_two_gain, g_two_bias, g_first, g_first_bias, g_inner_gain,
            g_inner_bias, g_second, g_second_bias)


def solution(mesh):
    devices = mesh.shape["wide"] * mesh.shape["narrow"]
    split, line, whole = P(AXES, None), P(AXES), P()
    return jax.shard_map(
        functools.partial(local, devices),
        mesh=mesh,
        in_specs=(split, split, split, whole, line, line, split, line, whole, split, split, line, line,
                  line, line, line, split, line, line, line, split, line),
        out_specs=(split, split, line, line, split, line, whole, split, split, line, line, line, line,
                   line, split, line, line, line, split, line),
        check_vma=False,
    )
```

time: 3300 us -> 995 us (0.30)
  other arithmetic: 1450 us -> 18.5 us
  local copies, waits for them, and re-layouts: 1030 us -> 30.5 us
  waiting for transfers between devices: 595 us -> 692 us
  Pallas kernels: 0 us -> 86.9 us
  matrix products: 113 us -> 68.9 us
    scatter-add x1 -> x0, other arithmetic: 1390 us -> none  [local(): jax.ops.segment_sum(jnp.transpose(bias_grad, (1, 2, 0)).reshape(seq * seq...]
    gather x2 -> x0, local copies, waits for them, and re-layouts: 934 us -> none  [local(): rel_bias = jnp.transpose(table.astype(f32)[buckets], (2, 0, 1))]
    all_gather x4, waiting for transfers between devices: 0.08 us -> 135 us  [gather(): return lax.all_gather(x, AXES, axis=0, tiled=True)]
    pallas_call x0 -> x2, Pallas kernels: none -> 86.9 us  [the longest x1 48.2 us: attention_backward(): pl.pallas_call(backward_kernel, grid=(pairs,), in_specs=[narrow(0), narro...]
    reshape x1 -> x20, local copies, waits for them, and re-layouts: 62.2 us -> 7.56 us  [the longest x3 4.21 us: unpack(): out.append(packed[:, at:at + size].reshape(-1))]
    unnamed x10, waiting for transfers between devices: 96.9 us -> 46.1 us
    dot_general x18 -> x12, matrix products: 113 us -> 68.9 us  [dot(): return lax.dot_general(a, b, dims, preferred_element_type=f32)]
    all_gather x1 -> x0, blocking collectives: 41.3 us -> none  [local(): lax.all_gather(rel_table, ('wide', 'narrow'), axis=0, tiled=True)]
  transfers between devices with their start and end apart: 9 -> 9, of which waited for: 5 -> 9; matrix products, arithmetic and copies ran while one was open for 32% -> 7% of each run, Pallas kernels for 0% -> 4%
where the time goes in v1:
time: 995 us; the launch traced here: 994 us
  waiting for transfers between devices  692 us (70%)
  Pallas kernels  86.9 us (9%)
  blocking collectives  81.9 us (8%)
  matrix products  68.9 us (7%)
  local copies, waits for them, and re-layouts  30.5 us (3%)
  other arithmetic  18.5 us (2%)
  between operations  14.3 us (1%)
    reduce_scatter x4, waiting for transfers between devices, scatter(): return lax.psum_scatter(x, AXES, scatter_dimension=0, tiled=True)  511 us
    all_gather x4, waiting for transfers between devices, gather(): return lax.all_gather(x, AXES, axis=0, tiled=True)  135 us
    dot_general x12, matrix products, dot(): return lax.dot_general(a, b, dims, preferred_element_type=f32)  68.9 us
    pallas_call x1, Pallas kernels, attention_backward(): pl.pallas_call(backward_kernel, grid=(pairs,), in_specs=[narrow(0), narro...  48.2 us
    unnamed x10, waiting for transfers between devices  46.1 us
    unnamed x1, blocking collectives  42.8 us
    psum x1, blocking collectives, local(): g_scale = lax.psum(g_scale, AXES)  39.1 us
    pallas_call x1, Pallas kernels, attention_forward(): pl.pallas_call(forward_kernel, grid=(pairs,), in_specs=[pl.BlockSpec((seq...  38.7 us
  transfers between devices with their start and end apart: 9, of which 9 were waited for; matrix products, arithmetic and copies ran while one was open for 7% of the time, Pallas kernels for 4%

profile of v1, /device:TPU:0, one launch (start us, length us, event | category | flops | bytes accessed | tf_op | source)
XLA Modules:
  0.0 993.7 jit_solution(15961720206777053643)
XLA Ops:
  7.3 0.7 all-gather.6.cloned.1.call-update
  8.0 0.7 all-gather.8.cloned.1.call-update
  8.7 0.7 all-gather.10.cloned.1.call-update
  9.5 0.5 all-gather.12.cloned.1.call-update
  10.1 0.8 reshape.308
  10.8 0.7 broadcast_in_dim.8
  11.6 8.1 concatenate.20
  19.7 0.2 dynamic-update-slice
  20.0 42.8 %all-reduce = bf16[19968]{0:T(1024)(128)(2,1)S(1)} all-reduce(bf16[19968]{0:T(1024)(128)(2,1)S(1)} %dynamic-update-slice), channel_id=2, replica_groups=mesh['wide'=8,'narrow'=4] {'wide','narrow'}, use_global_device_ids=true, to_apply=%add | all-reduce | flops 19968 | bytes 79872
  62.8 0.1 reshape.353
  64.3 0.6 reshape.340.table_ref
  64.9 0.9 copy.50.segc_ref
  65.8 0.2 convert_reduce_fusion.1
  66.0 0.4 fusion.21
  66.4 7.8 all-gather.6.cloned.1.call-done
  74.1 5.6 fusion.6.q_ref.k_ref.v_ref
  79.8 38.7 %attention_forward.1 = (f32[512,768]{1,0:T(8,128)}, bf16[12,512,512]{2,1,0:T(8,128)(2,1)}) custom-call(bf16[512,2304]{1,0:T(8,128)(2,1)} %fusion.6.q_ref.k_ref.v_ref, bf16[512,2304]{1,0:T(8,128)(2,1)} %fusion.6.q_ref.k_ref.v_ref, bf16[512,2304]{1,0:T(8,128)(2,1)} %fusion.6.q_ref.k_ref.v_ref, f32[6,2,256]{2,1,0:T(2,128)} %reshape.340.table_ref, ...), custom_call_target="tpu_custom_call" | custom-call | tf_op jit(solution)/shard_map/attention_forward/pallas_call | solution.py:72
  118.5 11.4 %all-gather.8.cloned.1.call-done = bf16[768,768]{1,0:T(8,128)(2,1)} async-done(((bf16[24,768]{1,0:T(8,128)(2,1)}), bf16[768,768]{1,0:T(8,128)(2,1)}) %all-gather.8.cloned.1.call-update) | async-done | bytes 1179664 | tf_op jit(solution)/shard_map/all_gather | solution.py:226
  129.8 2.6 fusion.34
  132.5 0.3 multiply_reduce_fusion.10
  132.8 0.8 copy-done.7
  133.6 0.6 fusion.31
  134.2 0.3 multiply_reduce_fusion.9
  134.5 60.8 %all-gather.10.cloned.1.call-done = bf16[768,3072]{1,0:T(8,128)(2,1)} async-done(((bf16[24,3072]{1,0:T(8,128)(2,1)}), bf16[768,3072]{1,0:T(8,128)(2,1)}) %all-gather.10.cloned.1.call-update) | async-done | bytes 4718608 | tf_op jit(solution)/shard_map/all_gather | solution.py:226
  195.3 6.8 fusion.30
  202.1 0.8 multiply_reduce_fusion.2
  202.9 1.8 copy-done
  204.8 55.2 %all-gather.12.cloned.1.call-done = bf16[3072,768]{1,0:T(8,128)(2,1)} async-done(((bf16[96,768]{1,0:T(8,128)(2,1)}), bf16[3072,768]{1,0:T(8,128)(2,1)}) %all-gather.12.cloned.1.call-update) | async-done | bytes 4718608 | tf_op jit(solution)/shard_map/all_gather | solution.py:226
  260.0 8.0 multiply_reduce_fusion
  268.0 8.7 convert_reduce_fusion
  276.7 6.5 multiply_reduce_fusion.5
  283.3 1.7 multiply_reduce_fusion.6
  285.0 0.5 convert_reduce_fusion.5
  285.5 0.6 copy-done.4
  286.1 0.9 copy-done.2
  286.9 0.6 copy-done.14
  287.6 1.7 multiply_reduce_fusion.4
  289.3 48.2 %attention_backward.1 = (bf16[512,768]{1,0:T(8,128)(2,1)}, bf16[512,768]{1,0:T(8,128)(2,1)}, bf16[512,768]{1,0:T(8,128)(2,1)}, f32[64,64]{1,0:T(8,128)}) custom-call(bf16[512,2304]{1,0:T(8,128)(2,1)} %fusion.6.q_ref.k_ref.v_ref, bf16[512,2304]{1,0:T(8,128)(2,1)} %fusion.6.q_ref.k_ref.v_ref, bf16[512,2304]{1,0:T(8,128)(2,1)} %fusion.6.q_ref.k_ref.v_ref, ...), custom_call_target="tpu_custom_call" | custom-call | tf_op jit(solution)/shard_map/attention_backward/pallas_call | solution.py:171
  337.4 1.4 convert_reduce_fusion.4
  338.8 2.2 constant_dynamic-update-slice_fusion.2
  341.3 0.1 convert_reduce_fusion.3
  342.3 1.0 constant_dynamic-update-slice_fusion.1
  343.3 1.0 constant_dynamic-update-slice_fusion
  344.3 6.2 fusion.20
  350.7 0.7 concatenate.26
  351.5 3.4 fusion.23
  354.9 0.3 reduce-scatter.5.cloned.1.call-start
  355.2 0.8 copy-done.9
  356.0 6.8 fusion.24
  362.9 7.2 fusion.27
  370.2 1.1 copy-done.16
  371.2 8.2 fusion.35
  379.7 39.1 %psum.7 = f32[12]{0:T(128)} all-reduce(f32[12]{0:T(128)S(1)} %reduce_sum.309), channel_id=1, replica_groups=mesh['wide'=8,'narrow'=4] {'wide','narrow'}, use_global_device_ids=true, to_apply=%region_33.0 | all-reduce | flops 12 | bytes 96 | tf_op jit(solution)/shard_map/psum | solution.py:307
  418.9 3.2 fusion.19
  422.1 5.8 add_convert_fusion.1
  428.0 43.5 %all-reduce.4.cloned.1.call-done = f32[32,624]{1,0:T(8,128)} async-done(((f32[32,624]{1,0:T(8,128)}), f32[32,624]{1,0:T(8,128)}) %all-reduce.4.cloned.1.call-update) | async-done | bytes 79888
  471.4 1.4 dynamic-slice_bitcast_fusion.1
  472.8 0.7 reshape_reshape.3
  473.5 1.3 dynamic-slice_bitcast_fusion.9
  474.7 1.6 dynamic-slice_bitcast_fusion
  476.3 102.6 %reduce-scatter.7.cloned.1.call-done = f32[24,768]{1,0:T(8,128)} async-done(((f32[768,768]{1,0:T(8,128)}), f32[24,768]{1,0:T(8,128)}) %reduce-scatter.7.cloned.1.call-update) | async-done | bytes 73744 | tf_op jit(solution)/shard_map/reduce_scatter | solution.py:230
  578.9 124.8 %reduce-scatter.5.cloned.1.call-done = f32[24,2304]{1,0:T(8,128)} async-done(((f32[768,2304]{1,0:T(8,128)}), f32[24,2304]{1,0:T(8,128)}) %reduce-scatter.5.cloned.1.call-update) | async-done | bytes 221200 | tf_op jit(solution)/shard_map/reduce_scatter | solution.py:230
  703.7 141.6 %reduce-scatter.9.cloned.1.call-done = f32[24,3072]{1,0:T(8,128)} async-done(((f32[768,3072]{1,0:T(8,128)}), f32[24,3072]{1,0:T(8,128)}) %reduce-scatter.9.cloned.1.call-update) | async-done | bytes 294928 | tf_op jit(solution)/shard_map/reduce_scatter | solution.py:230
  845.3 141.9 %reduce-scatter.11.cloned.1.call-done = f32[96,768]{1,0:T(8,128)} async-done(((f32[3072,768]{1,0:T(8,128)}), f32[96,768]{1,0:T(8,128)}) %reduce-scatter.11.cloned.1.call-update) | async-done | bytes 294928 | tf_op jit(solution)/shard_map/reduce_scatter | solution.py:230
  (102 shorter events, 3.5 us)
Async XLA Ops:
  7.2 57.7 %copy-start.19 = (s32[1,512]{1,0:T(1,128)S(1)}, s32[1,512]{1,0:T(1,128)}, u32[]{:S(2)}) copy-start(s32[1,512]{1,0:T(1,128)} %segr_ref.1) | copy-start | bytes 6148
  7.2 58.6 %copy-start.6 = (bf16[512,768]{1,0:T(8,128)(2,1)S(1)}, bf16[512,768]{1,0:T(8,128)(2,1)}, u32[]{:S(2)}) copy-start(bf16[512,768]{1,0:T(8,128)(2,1)} %param.22) | copy-start | bytes 2359300
  7.2 66.9 %all-gather.6.cloned.1.call-start = ((), (), s32[]{:S(2)}) async-start(), calls=%async_computation.4 | async-start | bytes 3649536 | tf_op jit(solution)/shard_map/all_gather | solution.py:226
  7.9 121.9 %all-gather.8.cloned.1.call-start = ((), (), s32[]{:S(2)}) async-start(), calls=%async_computation.5 | async-start | bytes 1216512 | tf_op jit(solution)/shard_map/all_gather | solution.py:226
  8.7 186.6 %all-gather.10.cloned.1.call-start = ((), (), s32[]{:S(2)}) async-start(), calls=%async_computation.6 | async-start | bytes 4866048 | tf_op jit(solution)/shard_map/all_gather | solution.py:226
  9.4 250.6 %all-gather.12.cloned.1.call-start = ((), (), s32[]{:S(2)}) async-start(), calls=%async_computation.7 | async-start | bytes 4866048 | tf_op jit(solution)/shard_map/all_gather | solution.py:226
  10.0 461.4 %all-reduce.4.cloned.1.call-start = ((), (), s32[]{:S(2)}) async-start(), calls=%async_computation.12 | async-start | bytes 163840
  132.4 1.1 copy-start.7
  202.1 2.6 copy-start
  260.0 8.0 copy-start.1
  276.7 6.5 copy-start.12
  276.7 6.5 copy-start.15
  284.9 1.1 copy-start.4
  285.0 2.0 copy-start.2
  285.0 2.6 copy-start.14
  286.1 3.2 copy-start.10
  337.4 3.9 copy-start.13
  337.4 4.6 copy-start.18
  338.8 3.5 copy-start.17
  342.3 2.0 copy-start.8
  344.3 7.2 copy-start.3
  351.5 227.4 %reduce-scatter.7.cloned.1.call-start = ((), (), s32[]{:S(2)}) async-start(), calls=%async_computation.9 | async-start | bytes 2433024 | tf_op jit(solution)/shard_map/reduce_scatter | solution.py:230
  354.9 1.1 copy-start.9
  354.9 348.8 %reduce-scatter.5.cloned.1.call-start = ((), (), s32[]{:S(2)}) async-start(), calls=%async_computation.8 | async-start | bytes 7299072 | tf_op jit(solution)/shard_map/reduce_scatter | solution.py:230
  362.8 482.5 %reduce-scatter.9.cloned.1.call-start = ((), (), s32[]{:S(2)}) async-start(), calls=%async_computation.10 | async-start | bytes 9732096 | tf_op jit(solution)/shard_map/reduce_scatter | solution.py:230
  370.1 1.1 copy-start.16
  370.1 617.1 %reduce-scatter.11.cloned.1.call-start = ((), (), s32[]{:S(2)}) async-start(), calls=%async_computation.11 | async-start | bytes 9732096 | tf_op jit(solution)/shard_map/reduce_scatter | solution.py:230
  379.4 39.4 %copy-start.5 = (f32[512,768]{1,0:T(8,128)S(1)}, f32[512,768]{1,0:T(8,128)}, u32[]{:S(2)}) copy-start(f32[512,768]{1,0:T(8,128)} %copy-done.4) | copy-start | bytes 4718596
  418.9 3.2 copy-start.11
Sparse Core Ops, SparseCore 0:
  10.9 63.1 all-gather.5
  77.0 52.7 all-gather.7
  132.8 62.5 all-gather.9
  198.1 61.8 all-gather.11
  351.6 119.7 all-reduce.3
  477.1 101.7 reduce-scatter.6
  585.1 118.5 reduce-scatter.4
  710.2 135.1 reduce-scatter.8
  851.8 135.3 reduce-scatter.10

commit v2 on v1

--- a/solution.py
+++ b/solution.py
@@ -192,6 +192,376 @@
     high, low = HIGH, hist.shape[1]
     return hist.reshape(high, 16, low)[:, :heads].transpose(0, 2, 1).reshape(high * low, heads)
 
+MESH = pl.DeviceIdType.MESH
+
+
+class Place:
+    def __init__(self):
+        wide, narrow = lax.axis_index("wide"), lax.axis_index("narrow")
+        self.z, self.x = wide // 2, wide % 2
+        self.y, self.c = narrow // 2, narrow % 2
+
+    def device(self, z=None, x=None, y=None, c=None):
+        z = self.z if z is None else z
+        x = self.x if x is None else x
+        y = self.y if y is None else y
+        c = self.c if c is None else c
+        return (z * 2 + x, y * 2 + c)
+
+    def peers(self):
+        out = [self.device(z=(self.z + d) % 4) for d in (1, 2, 3)]
+        return out + [self.device(x=1 - self.x), self.device(y=1 - self.y), self.device(c=1 - self.c)]
+
+    def greet(self):
+        barrier = pltpu.get_barrier_semaphore()
+        for peer in self.peers():
+            pl.semaphore_signal(barrier, inc=1, device_id=peer, device_id_type=MESH)
+        pl.semaphore_wait(barrier, 6)
+
+
+def send(src, dst, send_sem, recv_sem, to):
+    copy = pltpu.make_async_remote_copy(
+        src_ref=src, dst_ref=dst, send_sem=send_sem, recv_sem=recv_sem, device_id=to, device_id_type=MESH
+    )
+    copy.start()
+    return copy
+
+
+class Gather:
+    SLOTS = 35
+
+    def __init__(self, place, shard, whole, local_sem, send_sem, recv_sem):
+        self.p, self.shard, self.whole = place, shard, whole
+        self.local_sem, self.send_sem, self.recv_sem = local_sem, send_sem, recv_sem
+        width = shard.shape[-1]
+        self.half = (width // 256) * 128
+        self.sent, self.width = [], width
+
+    def at(self, z, x, y, c, part=None):
+        ref = self.whole.at[z, x, y, c]
+        if part == 0:
+            return ref.at[:, pl.ds(0, self.half)]
+        if part == 1:
+            return ref.at[:, pl.ds(self.half, self.width - self.half)]
+        return ref
+
+    def go(self, src, dst, slot, to):
+        self.sent.append(send(src, dst, self.send_sem.at[slot], self.recv_sem.at[slot], to))
+
+    def arrived(self, dst, slot):
+        pltpu.make_async_copy(dst, dst, self.recv_sem.at[slot]).wait()
+
+    def begin(self):
+        p = self.p
+        mine = self.at(p.z, p.x, p.y, p.c)
+        self.own = pltpu.make_async_copy(self.shard, mine, self.local_sem)
+        self.own.start()
+        for d in (1, 2, 3):
+            self.go(self.shard, mine, d - 1, p.device(z=(p.z + d) % 4))
+        self.go(self.shard, mine, 3, p.device(x=1 - p.x))
+        self.go(self.shard, mine, 7, p.device(y=1 - p.y))
+        self.go(self.shard, mine, 19, p.device(c=1 - p.c))
+
+    def line(self):
+        p = self.p
+        for d in (1, 2, 3):
+            ref = self.at((p.z + 4 - d) % 4, p.x, p.y, p.c)
+            self.arrived(ref, d - 1)
+            self.go(ref, ref, 3 + d, p.device(x=1 - p.x))
+            self.go(ref, ref, 7 + d, p.device(y=1 - p.y))
+            self.go(ref, ref, 19 + d, p.device(c=1 - p.c))
+
+    def cross(self):
+        p = self.p
+        for d in range(4):
+            z = (p.z + 4 - d) % 4
+            ref = self.at(z, 1 - p.x, p.y, p.c)
+            self.arrived(ref, 3 + d)
+            if self.half:
+                part = self.at(z, 1 - p.x, p.y, p.c, 0)
+                self.go(part, part, 11 + d, p.device(y=1 - p.y))
+            self.go(ref, ref, 23 + d, p.device(c=1 - p.c))
+            ref = self.at(z, p.x, 1 - p.y, p.c)
+            self.arrived(ref, 7 + d)
+            part = self.at(z, p.x, 1 - p.y, p.c, 1)
+            self.go(part, part, 15 + d, p.device(x=1 - p.x))
+            self.go(ref, ref, 27 + d, p.device(c=1 - p.c))
+
+    def corner(self):
+        p = self.p
+        for d in range(4):
+            z = (p.z + 4 - d) % 4
+            if self.half:
+                self.arrived(self.at(z, 1 - p.x, 1 - p.y, p.c, 0), 11 + d)
+            self.arrived(self.at(z, 1 - p.x, 1 - p.y, p.c, 1), 15 + d)
+            ref = self.at(z, 1 - p.x, 1 - p.y, p.c)
+            self.go(ref, ref, 31 + d, p.device(c=1 - p.c))
+
+    def finish(self):
+        p = self.p
+        other = 1 - p.c
+        for d in range(4):
+            z = (p.z + 4 - d) % 4
+            self.arrived(self.at(z, p.x, p.y, other), 19 + d)
+            self.arrived(self.at(z, 1 - p.x, p.y, other), 23 + d)
+            self.arrived(self.at(z, p.x, 1 - p.y, other), 27 + d)
+            self.arrived(self.at(z, 1 - p.x, 1 - p.y, other), 31 + d)
+
+    def drain(self):
+        self.own.wait()
+        for copy in self.sent:
+            copy.wait_send()
+
+
+def gather_kernel(count, *refs):
+    shards, wholes = refs[:count], refs[count : 2 * count]
+    local_sem, send_sem, recv_sem = refs[2 * count :]
+    place = Place()
+    place.greet()
+    jobs = [
+        Gather(place, shards[i], wholes[i], local_sem.at[i], send_sem.at[i], recv_sem.at[i])
+        for i in range(count)
+    ]
+    for job in jobs:
+        job.begin()
+    for step in range(count + 2):
+        if step < count:
+            jobs[step].line()
+        if 0 <= step - 1 < count:
+            jobs[step - 1].cross()
+        if 0 <= step - 2 < count:
+            jobs[step - 2].corner()
+    for job in jobs:
+        job.finish()
+    for job in jobs:
+        job.drain()
+
+
+def gather_all(shards, collective_id):
+    count = len(shards)
+    wholes = pl.pallas_call(
+        functools.partial(gather_kernel, count),
+        in_specs=[pl.BlockSpec(memory_space=pltpu.VMEM)] * count,
+        out_specs=[pl.BlockSpec(memory_space=pl.ANY)] * count,
+        out_shape=[jax.ShapeDtypeStruct((4, 2, 2, 2) + s.shape, s.dtype) for s in shards],
+        scratch_shapes=[
+            pltpu.SemaphoreType.DMA((count,)),
+            pltpu.SemaphoreType.DMA((count, Gather.SLOTS)),
+            pltpu.SemaphoreType.DMA((count, Gather.SLOTS)),
+        ],
+        compiler_params=pltpu.CompilerParams(collective_id=collective_id, has_side_effects=True),
+        name="gather_all",
+    )(*shards)
+    return [w.reshape(32 * s.shape[0], s.shape[1]) for w, s in zip(wholes, shards)]
+
+
+class Reduce:
+    SLOTS = 12
+
+    @staticmethod
+    def scratch(shape, dtype):
+        rows, width = shape
+        half = (width // 256) * 128
+        four = lambda w: pltpu.VMEM((4, rows, w), dtype)
+        return [
+            pltpu.VMEM((4, 4, rows, width), dtype),
+            pltpu.VMEM((4, 4, rows, width), dtype),
+            four(max(half, 128)), four(width - half), four(width), four(width),
+            pltpu.VMEM((3, rows, width), dtype),
+            pltpu.SemaphoreType.DMA((Reduce.SLOTS,)),
+            pltpu.SemaphoreType.DMA((Reduce.SLOTS,)),
+        ]
+
+    def __init__(self, place, parts, out, scratch):
+        self.p, self.parts, self.out = place, parts, out
+        (self.other, self.ready, self.by_y, self.by_x, self.from_x, self.from_y, self.from_z,
+         self.send_sem, self.recv_sem) = scratch
+        width = out.shape[-1]
+        self.half, self.width, self.sent = (width // 256) * 128, width, []
+
+    def go(self, src, dst, slot, to):
+        self.sent.append(send(src, dst, self.send_sem.at[slot], self.recv_sem.at[slot], to))
+
+    def arrived(self, dst, slot):
+        pltpu.make_async_copy(dst, dst, self.recv_sem.at[slot]).wait()
+
+    def spots(self):
+        p = self.p
+        return [(1 - p.x, 1 - p.y), (1 - p.x, p.y), (p.x, 1 - p.y), (p.x, p.y)]
+
+    def begin(self):
+        p = self.p
+        for i, (x, y) in enumerate(self.spots()):
+            self.go(self.parts.at[:, x, y, 1 - p.c], self.other.at[i], i, p.device(c=1 - p.c))
+
+    def pair(self, i, z):
+        x, y = self.spots()[i]
+        return self.parts[z, x, y, self.p.c].astype(f32) + self.other[i, z].astype(f32)
+
+    def corner(self):
+        p, half = self.p, self.half
+        self.arrived(self.other.at[0], 0)
+
+        @pl.loop(0, 4)
+        def _(z):
+            self.ready[0, z] = self.pair(0, z).astype(self.ready.dtype)
+
+        if half:
+            self.go(self.ready.at[0, :, :, pl.ds(0, half)], self.by_y, 4, p.device(y=1 - p.y))
+        self.go(self.ready.at[0, :, :, pl.ds(half, self.width - half)], self.by_x, 5, p.device(x=1 - p.x))
+
+    def cross(self):
+        p, half = self.p, self.half
+        self.arrived(self.other.at[1], 1)
+        if half:
+            self.arrived(self.by_y, 4)
+
+        @pl.loop(0, 4)
+        def _(z):
+            total = self.pair(1, z)
+            if half:
+                total = jnp.concatenate([total[:, :half] + self.by_y[z].astype(f32), total[:, half:]], axis=1)
+            self.ready[1, z] = total.astype(self.ready.dtype)
+
+        self.go(self.ready.at[1], self.from_x, 6, p.device(x=1 - p.x))
+        self.arrived(self.other.at[2], 2)
+        self.arrived(self.by_x, 5)
+
+        @pl.loop(0, 4)
+        def _(z):
+            total = self.pair(2, z)
+            right = total[:, half:] + self.by_x[z].astype(f32)
+            total = jnp.concatenate([total[:, :half], right], axis=1) if half else right
+            self.ready[2, z] = total.astype(self.ready.dtype)
+
+        self.go(self.ready.at[2], self.from_y, 7, p.device(y=1 - p.y))
+
+    def line(self):
+        p = self.p
+        self.arrived(self.other.at[3], 3)
+        self.arrived(self.from_x, 6)
+        self.arrived(self.from_y, 7)
+        for d in (1, 2, 3):
+            z = (p.z + d) % 4
+            total = self.pair(3, z) + self.from_x[z].astype(f32) + self.from_y[z].astype(f32)
+            self.ready[3, z] = total.astype(self.ready.dtype)
+            self.go(self.ready.at[3, z], self.from_z.at[d - 1], 7 + d, p.device(z=z))
+
+    def finish(self):
+        p = self.p
+        for d in (1, 2, 3):
+            self.arrived(self.from_z.at[d - 1], 7 + d)
+        total = self.pair(3, p.z) + self.from_x[p.z].astype(f32) + self.from_y[p.z].astype(f32)
+        for d in (1, 2, 3):
+            total = total + self.from_z[d - 1].astype(f32)
+        self.out[...] = total
+
+    def drain(self):
+        for copy in self.sent:
+            copy.wait_send()
+
+
+class Everywhere:
+    @staticmethod
+    def scratch(shape):
+        return [pltpu.VMEM((3,) + shape, f32), pltpu.VMEM((6,) + shape, f32),
+                pltpu.SemaphoreType.DMA((6,)), pltpu.SemaphoreType.DMA((6,))]
+
+    def __init__(self, place, block, out, scratch):
+        self.p, self.block, self.out, self.sent = place, block, out, []
+        self.mine, self.got, self.send_sem, self.recv_sem = scratch
+
+    def go(self, src, slot, to):
+        self.sent.append(send(src, self.got.at[slot], self.send_sem.at[slot], self.recv_sem.at[slot], to))
+
+    def arrived(self, slot):
+        dst = self.got.at[slot]
+        pltpu.make_async_copy(dst, dst, self.recv_sem.at[slot]).wait()
+
+    def begin(self):
+        self.go(self.block, 0, self.p.device(c=1 - self.p.c))
+
+    def corner(self):
+        self.arrived(0)
+        self.mine[0] = self.block[...] + self.got[0]
+        self.go(self.mine.at[0], 1, self.p.device(x=1 - self.p.x))
+
+    def cross(self):
+        self.arrived(1)
+        self.mine[1] = self.mine[0] + self.got[1]
+        self.go(self.mine.at[1], 2, self.p.device(y=1 - self.p.y))
+
+    def line(self):
+        p = self.p
+        self.arrived(2)
+        self.mine[2] = self.mine[1] + self.got[2]
+        for d in (1, 2, 3):
+            self.go(self.mine.at[2], 2 + d, p.device(z=(p.z + d) % 4))
+
+    def finish(self):
+        p = self.p
+        for d in (1, 2, 3):
+            self.arrived(2 + d)
+        total = None
+        for z in range(4):
+            term = jnp.where(p.z == z, self.mine[2], 0.0)
+            for d in (1, 2, 3):
+                term = term + jnp.where((p.z + 4 - d) % 4 == z, self.got[2 + d], 0.0)
+            total = term if total is None else total + term
+        self.out[...] = total
+
+    def drain(self):
+        for copy in self.sent:
+            copy.wait_send()
+
+
+def reduce_kernel(count, extra, *refs):
+    total = count + extra
+    parts, outs, scratch = refs[:total], refs[total : 2 * total], refs[2 * total :]
+    place = Place()
+    place.greet()
+    jobs = [Reduce(place, parts[i], outs[i], scratch[9 * i : 9 * i + 9]) for i in range(count)]
+    if extra:
+        jobs.append(Everywhere(place, parts[count], outs[count], scratch[9 * count :]))
+    for job in jobs:
+        job.begin()
+    for step in range(total + 2):
+        if step < total:
+            jobs[step].corner()
+        if 0 <= step - 1 < total:
+            jobs[step - 1].cross()
+        if 0 <= step - 2 < total:
+            jobs[step - 2].line()
+    for job in jobs:
+        job.finish()
+    for job in jobs:
+        job.drain()
+
+
+def reduce_all(parts, block, collective_id):
+    shapes = [(p.shape[0] // 32, p.shape[1]) for p in parts]
+    given = [p.reshape((4, 2, 2, 2) + s) for p, s in zip(parts, shapes)]
+    outs = [jax.ShapeDtypeStruct(s, f32) for s in shapes]
+    scratch = []
+    for p, s in zip(parts, shapes):
+        scratch += Reduce.scratch(s, p.dtype)
+    extra = block is not None
+    if extra:
+        given.append(block)
+        outs.append(jax.ShapeDtypeStruct(block.shape, f32))
+        scratch += Everywhere.scratch(block.shape)
+    return pl.pallas_call(
+        functools.partial(reduce_kernel, len(parts), int(extra)),
+        in_specs=[pl.BlockSpec(memory_space=pltpu.VMEM)] * len(given),
+        out_specs=[pl.BlockSpec(memory_space=pltpu.VMEM)] * len(outs),
+        out_shape=outs,
+        scratch_shapes=scratch,
+        compiler_params=pltpu.CompilerParams(
+            collective_id=collective_id, has_side_effects=True, vmem_limit_bytes=60 * 2**20
+        ),
+        name="reduce_all",
+    )(*given)
+
 AXES = ("wide", "narrow")
 
 
@@ -222,15 +592,41 @@
     return out
 
 
-def gather(x):
-    return lax.all_gather(x, AXES, axis=0, tiled=True)
-
-
-def scatter(x):
-    return lax.psum_scatter(x, AXES, scatter_dimension=0, tiled=True)
-
-
-def local(devices, tokens, cotangent, segments, buckets, norm1_gain, norm1_bias, qkv_weight, qv_bias,
+def fill(x, count):
+    return jnp.pad(x, ((0, 0), (0, count - x.shape[1])))
+
+
+class Plain:
+    held = f32
+
+    @staticmethod
+    def gather(shards, small):
+        return [lax.all_gather(x, AXES, axis=0, tiled=True) for x in (*shards, small)]
+
+    @staticmethod
+    def reduce(parts, small, block):
+        sums = [lax.psum_scatter(x, AXES, scatter_dimension=0, tiled=True) for x in (*parts, small)]
+        return sums, lax.psum(block, AXES)
+
+
+class Direct:
+    held = bf16
+
+    @staticmethod
+    def gather(shards, small):
+        tiles = fill(small, 1024).reshape(8, 128)
+        *wholes, tiles = gather_all([*shards, tiles], 0)
+        return [*wholes, tiles.reshape(32, 1024)]
+
+    @staticmethod
+    def reduce(parts, small, block):
+        tiles = fill(small, 1024).reshape(256, 128)
+        line = fill(block[None, :], 1024).reshape(8, 128)
+        *sums, tiles, line = reduce_all([*parts, tiles], line, 1)
+        return [*sums, tiles.reshape(1, 1024)], line.reshape(-1)[: block.shape[0]]
+
+
+def local(devices, ways, tokens, cotangent, segments, buckets, norm1_gain, norm1_bias, qkv_weight, qv_bias,
           head_scale, rel_table, out_weight, out_bias, post_gain, post_bias, norm2_gain, norm2_bias,
           fc1_weight, fc1_bias, inner_gain, inner_bias, fc2_weight, fc2_bias):
     seq, width = tokens.shape
@@ -240,11 +636,8 @@
              qv_bias, fc1_bias, inner_gain, inner_bias, rel_table.reshape(-1))
     sizes = [v.shape[0] for v in small]
     nb = rel_table.shape[0] * devices
-    packed = gather(jnp.concatenate(small)[None, :])
-    w_qkv = gather(qkv_weight)
-    w_out = gather(out_weight)
-    w_first = gather(fc1_weight)
-    w_second = gather(fc2_weight)
+    w_qkv, w_out, w_first, w_second, packed = ways.gather(
+        (qkv_weight, out_weight, fc1_weight, fc2_weight), jnp.concatenate(small)[None, :])
     (gain_one, bias_one, bias_out, gain_post, bias_post, gain_two, bias_two, bias_second,
      bias_qv, bias_first, gain_inner, bias_inner, table) = [v.astype(f32) for v in unpack(packed, sizes)]
     table_t = table.reshape(nb, heads).T.reshape(heads // 2, 2, nb)
@@ -269,7 +662,7 @@
     output = (first + (dot(hidden, w_second) + bias_second)).astype(bf16)
 
     grad_out = cotangent.astype(f32)
-    g_second = scatter(dot(hidden, cotangent, TN))
+    g_second = dot(hidden, cotangent, TN).astype(ways.held)
     g_second_bias = jnp.sum(grad_out, axis=0)
     d_hidden = dot(cotangent, w_second, NT)
     g_inner_gain = jnp.sum(d_hidden * hat_inner, axis=0)
@@ -278,7 +671,7 @@
     pdf = jnp.exp(-0.5 * inner * inner) * (1.0 / math.sqrt(2.0 * math.pi))
     d_inner = (d_gelu * (cdf + inner * pdf)).astype(bf16)
     g_first_bias = jnp.sum(d_inner.astype(f32), axis=0)
-    g_first = scatter(dot(h_two, d_inner, TN))
+    g_first = dot(h_two, d_inner, TN).astype(ways.held)
     d_two = dot(d_inner, w_first, NT)
     g_two_gain = jnp.sum(d_two * hat_two, axis=0)
     g_two_bias = jnp.sum(d_two, axis=0)
@@ -287,7 +680,7 @@
     g_post_bias = jnp.sum(d_first, axis=0)
     d_mixed = norm_back(d_first, hat_post, inv_post, gain_post).astype(bf16)
     g_out_bias = jnp.sum(d_mixed.astype(f32), axis=0)
-    g_out = scatter(dot(scaled, d_mixed, TN))
+    g_out = dot(scaled, d_mixed, TN).astype(ways.held)
     d_scaled = dot(d_mixed, w_out, NT)
     g_scale = jnp.sum(jnp.sum(d_scaled * attn, axis=0).reshape(heads, size), axis=1)
     d_attn = (d_scaled * scale).astype(bf16)
@@ -295,7 +688,7 @@
     g_table = table_gradient(hist, heads)
     dqkv = jnp.concatenate([dq, dk, dv], axis=1)
     g_qv = jnp.concatenate([jnp.sum(dq.astype(f32), axis=0), jnp.sum(dv.astype(f32), axis=0)])
-    g_qkv = scatter(dot(h_one, dqkv, TN))
+    g_qkv = dot(h_one, dqkv, TN).astype(ways.held)
     d_one = dot(dqkv, w_qkv, NT)
     g_one_gain = jnp.sum(d_one * hat_one, axis=0)
     g_one_bias = jnp.sum(d_one, axis=0)
@@ -303,8 +696,8 @@
 
     grads = (g_one_gain, g_one_bias, g_out_bias, g_post_gain, g_post_bias, g_two_gain, g_two_bias,
              g_second_bias, g_qv, g_first_bias, g_inner_gain, g_inner_bias, g_table.reshape(-1))
-    summed = scatter(pack(grads, devices))
-    g_scale = lax.psum(g_scale, AXES)
+    (g_qkv, g_out, g_first, g_second, summed), g_scale = ways.reduce(
+        (g_qkv, g_out, g_first, g_second), pack(grads, devices), g_scale)
     (g_one_gain, g_one_bias, g_out_bias, g_post_gain, g_post_bias, g_two_gain, g_two_bias,
      g_second_bias, g_qv, g_first_bias, g_inner_gain, g_inner_bias, g_table) = unpack(summed, sizes)
     g_table = g_table.reshape(rel_table.shape)
@@ -315,9 +708,10 @@
 
 def solution(mesh):
     devices = mesh.shape["wide"] * mesh.shape["narrow"]
+    direct = (mesh.shape["wide"], mesh.shape["narrow"]) == (8, 4)
     split, line, whole = P(AXES, None), P(AXES), P()
     return jax.shard_map(
-        functools.partial(local, devices),
+        functools.partial(local, devices, Direct if direct else Plain),
         mesh=mesh,
         in_specs=(split, split, split, whole, line, line, split, line, whole, split, split, line, line,
                   line, line, line, split, line, line, line, split, line),

time: 995 us -> 362 us (0.36)
  waiting for transfers between devices: 692 us -> 0 us
  Pallas kernels: 86.9 us -> 248 us
  blocking collectives: 81.9 us -> 0 us
  matrix products: 68.9 us -> 52.7 us
  between operations: 14.3 us -> 1.15 us
    reduce_scatter x4 -> x0, waiting for transfers between devices: 511 us -> none  [scatter(): return lax.psum_scatter(x, AXES, scatter_dimension=0, tiled=True)]
    pallas_call x0 -> x2, Pallas kernels: none -> 160 us  [the longest x1 88.1 us: reduce_all(): pl.pallas_call(functools.partial(reduce_kernel, len(parts), int(extra)),...]
    all_gather x4 -> x0, waiting for transfers between devices: 135 us -> none  [gather(): return lax.all_gather(x, AXES, axis=0, tiled=True)]
    unnamed x10 -> x0, waiting for transfers between devices: 46.1 us -> none
    unnamed x1 -> x0, blocking collectives: 42.8 us -> none
    psum x1 -> x0, blocking collectives: 39.1 us -> none  [local(): g_scale = lax.psum(g_scale, AXES)]
    dot_general x12, matrix products: 68.9 us -> 52.7 us  [dot(): return lax.dot_general(a, b, dims, preferred_element_type=f32)]
  transfers between devices with their start and end apart: 9 -> 0, of which waited for: 9 -> 0; matrix products, arithmetic and copies ran while one was open for 7% -> 0% of each run, Pallas kernels for 4% -> 0%
where the time goes in v2:
time: 362 us; the launch traced here: 361 us
  Pallas kernels  248 us (69%)
  matrix products  52.7 us (15%)
  local copies, waits for them, and re-layouts  34.6 us (10%)
  other arithmetic  24.7 us (7%)
    pallas_call x1, Pallas kernels, reduce_all(): pl.pallas_call(functools.partial(reduce_kernel, len(parts), int(extra)),...  88.1 us
    pallas_call x1, Pallas kernels, gather_all(): pl.pallas_call(functools.partial(gather_kernel, count), in_specs=[pl.Bloc...  72.3 us
    dot_general x12, matrix products, dot(): return lax.dot_general(a, b, dims, preferred_element_type=f32)  52.7 us
    pallas_call x1, Pallas kernels, attention_backward(): pl.pallas_call(backward_kernel, grid=(pairs,), in_specs=[narrow(0), narro...  48.2 us
    pallas_call x1, Pallas kernels, attention_forward(): pl.pallas_call(forward_kernel, grid=(pairs,), in_specs=[pl.BlockSpec((seq...  39 us
    unnamed x68, local copies, waits for them, and re-layouts  14.5 us
    reduce_sum x1, other arithmetic, local(): g_first_bias = jnp.sum(d_inner.astype(f32), axis=0)  11.1 us
    concatenate x1, local copies, waits for them, and re-layouts, local(): jnp.concatenate(small)[None, :]  8.09 us

profile of v2, /device:TPU:0, one launch (start us, length us, event | category | flops | bytes accessed | tf_op | source)
XLA Modules:
  0.0 360.7 jit_solution(4459909939470634702)
XLA Ops:
  0.7 0.8 reshape.344
  1.5 8.1 %concatenate.20 = bf16[624]{0:T(1024)(128)(2,1)S(1)} concatenate(bf16[24]{0:T(256)(128)(2,1)} %param.26, bf16[24]{0:T(256)(128)(2,1)} %param.27, bf16[24]{0:T(256)(128)(2,1)} %param.33, bf16[24]{0:T(256)(128)(2,1)} %param.34, bf16[24]{0:T(256)(128)(2,1)} %param.35, bf16[24]{0:T(256)(128)(2,1)} %param.36, bf16[24]{0:T(256)(128)(2,1)} %param.37, bf16[24]{0:T(256)(128)(2,1)} %param.43, ...), dimensions={0} | concatenate | bytes 2496 | tf_op jit(solution)/shard_map/concatenate | solution.py:640
  9.6 0.6 pad_reduce_fusion
  10.2 1.4 convert_reduce_fusion.1
  11.6 1.5 fusion.23
  13.2 0.9 copy.47.segc_ref
  14.1 72.3 %gather_all.1 = (bf16[4,2,2,2,24,2304]{5,4,3,2,1,0:T(8,128)(2,1)}, bf16[4,2,2,2,24,768]{5,4,3,2,1,0:T(8,128)(2,1)}, bf16[4,2,2,2,24,3072]{5,4,3,2,1,0:T(8,128)(2...) custom-call(bf16[24,2304]{1,0:T(8,128)(2,1)} %refs_0_.1, bf16[24,768]{1,0:T(8,128)(2,1)} %refs_1_.1, ...), custom_call_target="tpu_custom_call" | custom-call | tf_op jit(solution)/shard_map/gather_all/pallas_call | solution.py:342
  86.4 0.9 copy.53
  87.5 0.1 slice_convert_fusion.2
  87.7 0.1 slice_convert_fusion
  87.9 0.1 reshape.397
  87.9 0.1 reshape.392
  88.0 0.1 reshape.385
  88.1 0.1 reshape.390
  88.5 0.1 reshape.400
  88.7 0.6 reshape.388.table_ref
  89.3 5.6 %fusion.8.q_ref.k_ref.v_ref = bf16[512,2304]{1,0:T(8,128)(2,1)} fusion(bf16[768,2304]{1,0:T(8,128)(2,1)} %bitcast.108, f32[2304]{0:T(1024)S(1)} %pad_maximum_fusion.1, bf16[512,768]{1,0:T(8,128)(2,1)S(1)} %copy-done.5, f32[768]{0:T(1024)S(1)} %reshape.386, f32[768]{0:T(1024)S(1)} %reshape.385, f32[512]{0:T(512)S(1)} %add_rsqrt_fusion.3, ...), kind=kOutput, calls=%fused_computation.22 | convolution fusion | flops 1816657920 | bytes 6704128 | tf_op jit(solution)/shard_map/dot_general | solution.py:17
  94.9 39.0 %attention_forward.1 = (f32[512,768]{1,0:T(8,128)}, bf16[12,512,512]{2,1,0:T(8,128)(2,1)}) custom-call(bf16[512,2304]{1,0:T(8,128)(2,1)} %fusion.8.q_ref.k_ref.v_ref, bf16[512,2304]{1,0:T(8,128)(2,1)} %fusion.8.q_ref.k_ref.v_ref, bf16[512,2304]{1,0:T(8,128)(2,1)} %fusion.8.q_ref.k_ref.v_ref, f32[6,2,256]{2,1,0:T(2,128)} %reshape.388.table_ref, ...), custom_call_target="tpu_custom_call" | custom-call | tf_op jit(solution)/shard_map/attention_forward/pallas_call | solution.py:72
  134.0 2.3 fusion.33
  136.3 0.3 multiply_reduce_fusion.8
  136.6 0.8 copy-done.6
  137.4 0.6 fusion.30
  138.0 0.3 multiply_reduce_fusion.7
  138.3 7.0 %fusion.29 = (f32[512]{0:T(512)S(1)}, f32[512,3072]{1,0:T(8,128)S(1)}, f32[512,3072]{1,0:T(8,128)}) fusion(f32[3072]{0:T(1024)S(1)} %reshape.394, bf16[768,3072]{1,0:T(8,128)(2,1)} %bitcast.102, f32[512,768]{1,0:T(8,128)S(1)} %get-tuple-element.77, f32[768]{0:T(1024)S(1)} %reshape.393, f32[768]{0:T(1024)S(1)} %reshape.392, f32[512]{0:T(512)S(1)} %add_rsqrt_fusion.1, ...), kind=kOutput, calls=%fused_computation.117 | convolution fusion | flops 2427321856 | bytes 18898944 | tf_op jit(solution)/shard_map/dot_general | solution.py:17
  145.3 0.8 multiply_reduce_fusion.1
  146.1 1.8 copy-done
  147.9 5.3 %fusion.6 = (f32[3072]{0:T(1024)S(1)}, f32[512]{0:T(512)S(1)}, f32[512]{0:T(512)S(1)}, f32[3072,512]{0,1:T(8,128)}) fusion(f32[512,3072]{1,0:T(8,128)S(1)} %get-tuple-element.75, f32[512]{0:T(512)S(1)} %add_rsqrt_fusion, f32[512]{0:T(512)S(1)} %broadcast_multiply_fusion.2, f32[3072]{0:T(1024)S(1)} %reshape.395, bf16[3072,768]{1,0:T(8,128)(2,1)S(1)} %bitcast.107, ...), kind=kOutput, calls=%fused_computation.9 | convolution fusion | flops 2428497920 | bytes 18120704 | tf_op jit(solution)/shard_map/dot_general | solution.py:17
  153.3 11.1 %convert_reduce_fusion = (f32[3072]{0:T(1024)S(1)}, bf16[512,3072]{1,0:T(8,128)(2,1)}, bf16[512,3072]{1,0:T(8,128)(2,1)}) fusion(f32[512,3072]{1,0:T(8,128)} %get-tuple-element.110, f32[3072]{0:T(1024)S(1)} %reshape.394, f32[512]{0:T(512)S(1)} %get-tuple-element.114, f32[512,3072]{1,0:T(8,128)} %copy-done, f32[512]{0:T(512)S(1)} %broadcast_multiply_fusion.2, ...), kind=kLoop, calls=%fused_computation.10 | loop fusion | flops 36172800 | bytes 25223168 | tf_op jit(solution)/shard_map/reduce_sum | solution.py:673
  164.4 3.1 reduce_sum.307
  167.5 6.9 %add_convert_fusion.1 = bf16[512,768]{1,0:T(8,128)(2,1)} fusion(f32[512,768]{1,0:T(8,128)S(1)} %get-tuple-element.77, bf16[512,3072]{1,0:T(8,128)(2,1)} %get-tuple-element.78, bf16[3072,768]{1,0:T(8,128)(2,1)} %bitcast.104, f32[768]{0:T(1024)S(1)} %reshape.397), kind=kOutput, calls=%fused_computation.54 | convolution fusion | flops 2417098752 | bytes 10226688 | tf_op jit(solution)/shard_map/dot_general | solution.py:17
  174.4 6.4 %multiply_reduce_fusion.3 = (f32[768]{0:T(1024)S(1)}, f32[512]{0:T(512)S(1)}, f32[512]{0:T(512)S(1)}, f32[768]{0:T(1024)S(1)}, f32[512,768]{1,0:T(8,128)}) fusion(f32[512,768]{1,0:T(8,128)S(1)} %get-tuple-element.77, f32[512]{0:T(512)S(1)} %add_rsqrt_fusion.1, f32[512]{0:T(512)S(1)} %broadcast_multiply_fusion.9, f32[768]{0:T(1024)S(1)} %reshape.392, ...), kind=kOutput, calls=%fused_computation.47 | convolution fusion | flops 2419455488 | bytes 11027456 | tf_op jit(solution)/shard_map/dot_general | solution.py:17
  180.9 0.1 reshape.362
  181.0 3.0 multiply_reduce_fusion.4
  184.1 4.9 %convolution_convert_fusion.1 = bf16[768,3072]{1,0:T(8,128)(2,1)} fusion(bf16[512,3072]{1,0:T(8,128)(2,1)S(1)} %copy-done.12, f32[512,768]{1,0:T(8,128)S(1)} %get-tuple-element.77, f32[768]{0:T(1024)S(1)} %reshape.393, f32[768]{0:T(1024)S(1)} %reshape.392, f32[512]{0:T(512)S(1)} %add_rsqrt_fusion.1, f32[512]{0:T(512)S(1)} %broadcast_multiply_fusion.9), kind=kOutput, calls=%fused_computation.19 | convolution fusion | flops 2420244480 | bytes 9447424 | tf_op jit(solution)/shard_map/dot_general | solution.py:17
  189.0 0.5 convert_reduce_fusion.5
  189.6 0.8 copy-done.1
  190.4 0.6 copy-done.17
  191.0 1.7 multiply_reduce_fusion.2
  192.8 48.2 %attention_backward.1 = (bf16[512,768]{1,0:T(8,128)(2,1)}, bf16[512,768]{1,0:T(8,128)(2,1)}, bf16[512,768]{1,0:T(8,128)(2,1)}, f32[64,64]{1,0:T(8,128)}) custom-call(bf16[512,2304]{1,0:T(8,128)(2,1)} %fusion.8.q_ref.k_ref.v_ref, bf16[512,2304]{1,0:T(8,128)(2,1)} %fusion.8.q_ref.k_ref.v_ref, bf16[512,2304]{1,0:T(8,128)(2,1)} %fusion.8.q_ref.k_ref.v_ref, ...), custom_call_target="tpu_custom_call" | custom-call | tf_op jit(solution)/shard_map/attention_backward/pallas_call | solution.py:171
  241.0 1.9 convolution_convert_fusion.3
  242.8 0.1 convert_reduce_fusion.4
  243.1 0.1 convert_reduce_fusion.3
  243.4 0.1 reduce_sum.309
  243.5 0.6 pad.14
  244.5 0.1 copy.49
  244.7 0.1 reshape_reshape_reshape.3
  245.0 1.8 copy-done.26
  246.8 0.2 copy-done.7
  247.0 2.3 fusion.22
  249.4 1.4 fusion.21
  251.0 0.1 concatenate.26
  251.2 0.7 copy.51
  251.8 4.1 %convolution_convert_fusion.2 = bf16[768,2304]{1,0:T(8,128)(2,1)} fusion(bf16[512,2304]{1,0:T(8,128)(2,1)S(1)} %copy-done.22, bf16[512,768]{1,0:T(8,128)(2,1)S(1)} %copy-done.7, f32[768]{0:T(1024)S(1)} %reshape.386, f32[768]{0:T(1024)S(1)} %reshape.385, f32[512]{0:T(512)S(1)} %add_rsqrt_fusion.3, f32[512]{0:T(512)S(1)} %broadcast_multiply_fusion.11), kind=kOutput, calls=%fused_computation.20 | convolution fusion | flops 1816068096 | bytes 6694912 | tf_op jit(solution)/shard_map/dot_general | solution.py:17
  255.9 4.3 %convolution_convert_fusion = bf16[3072,768]{1,0:T(8,128)(2,1)} fusion(bf16[512,3072]{1,0:T(8,128)(2,1)S(1)} %copy-done.10, bf16[512,768]{1,0:T(8,128)(2,1)S(1)} %copy-done.19), kind=kOutput, calls=%fused_computation.18 | convolution fusion | flops 2418278400 | bytes 8650752 | tf_op jit(solution)/shard_map/dot_general | solution.py:17
  260.2 88.1 %reduce_all.1 = (f32[24,2304]{1,0:T(8,128)}, f32[24,768]{1,0:T(8,128)}, f32[24,3072]{1,0:T(8,128)}, f32[96,768]{1,0:T(8,128)}, f32[8,128]{1,0:T(8,128)}, /*index=5*/f32[8,128]{1,0:T(8,128)}) custom-call(bf16[4,2,2,2,24,2304]{5,4,3,2,1,0:T(8,128)(2,1)} %bitcast.84, bf16[4,2,2,2,24,768]{5,4,3,2,1,0:T(8,128)(2,1)} %bitcast.83, ...), custom_call_target="tpu_custom_call" | custom-call | tf_op jit(solution)/shard_map/reduce_all/pallas_call | solution.py:553
  348.3 1.2 slice_bitcast_fusion.9
  349.5 1.2 slice.117
  350.7 1.3 slice_bitcast_fusion.1
  352.0 1.5 slice_bitcast_fusion
  353.5 0.7 reshape_reshape.11
  354.2 1.6 copy.60
  355.8 1.5 copy.61
  357.4 1.7 copy.62
  359.0 1.7 copy.63
  (103 shorter events, 2.3 us)
Async XLA Ops:
  0.7 12.6 %copy-start.24 = (s32[1,512]{1,0:T(1,128)S(1)}, s32[1,512]{1,0:T(1,128)}, u32[]{:S(2)}) copy-start(s32[1,512]{1,0:T(1,128)} %segr_ref.1) | copy-start | bytes 6148
  0.7 12.4 %copy-start.25 = (bf16[12]{0:T(256)(128)(2,1)S(1)}, bf16[12]{0:T(256)(128)(2,1)}, u32[]{:S(2)}) copy-start(bf16[12]{0:T(256)(128)(2,1)} %param.30) | copy-start | bytes 76
  10.2 79.2 %copy-start.5 = (bf16[512,768]{1,0:T(8,128)(2,1)S(1)}, bf16[512,768]{1,0:T(8,128)(2,1)}, u32[]{:S(2)}) copy-start(bf16[512,768]{1,0:T(8,128)(2,1)} %param.22) | copy-start | bytes 2359300
  94.9 39.0 %copy-start.16 = (bf16[4,2,2,2,24,768]{5,4,3,2,1,0:T(8,128)(2,1)S(1)}, bf16[4,2,2,2,24,768]{5,4,3,2,1,0:T(8,128)(2,1)}, u32[]{:S(2)}) copy-start(bf16[4,2,2,2,24,768]{5,4,3,2,1,0:T(8,128)(2,1)} %get-tuple-element.40) | copy-start | bytes 3538948
  136.3 1.1 copy-start.6
  138.0 9.9 %slice-start = ((s8[4718592]{0:T(1024)(128)(4,1)}), s8[4194304]{0:T(1024)(128)(4,1)S(1)}, s32[]{:S(2)}) async-start(s8[4718592]{0:T(1024)(128)(4,1)} %bitcast.105), calls=%async_computation | async-start | bytes 8388608
  138.3 9.6 %slice-start.1 = ((s8[4718592]{0:T(1024)(128)(4,1)}), s8[524288]{0:T(1024)(128)(4,1)S(1)}, s32[]{:S(2)}) async-start(s8[4718592]{0:T(1024)(128)(4,1)} %bitcast.105), calls=%async_computation.1 | async-start | bytes 1048576
  145.3 2.6 copy-start
  145.3 2.6 copy-start.18
  167.5 6.9 %copy-start.11 = (bf16[512,3072]{1,0:T(8,128)(2,1)S(1)}, bf16[512,3072]{1,0:T(8,128)(2,1)}, u32[]{:S(2)}) copy-start(bf16[512,3072]{1,0:T(8,128)(2,1)} %get-tuple-element.70) | copy-start | bytes 9437188
  181.0 3.0 copy-start.12
  184.1 4.9 %copy-start.3 = (f32[512,768]{1,0:T(8,128)}, f32[512,768]{1,0:T(8,128)S(1)}, u32[]{:S(2)}) copy-start(f32[512,768]{1,0:T(8,128)S(1)} %get-tuple-element.73) | copy-start | bytes 4718596
  189.0 1.4 copy-start.1
  189.0 2.0 copy-start.17
  189.6 3.2 copy-start.8
  192.8 48.2 %copy-start.2 = (f32[512,768]{1,0:T(8,128)S(1)}, f32[512,768]{1,0:T(8,128)}, u32[]{:S(2)}) copy-start(f32[512,768]{1,0:T(8,128)} %get-tuple-element.39.attn_ref) | copy-start | bytes 4718596
  192.8 48.2 %copy-start.9 = (bf16[512,768]{1,0:T(8,128)(2,1)S(1)}, bf16[512,768]{1,0:T(8,128)(2,1)}, u32[]{:S(2)}) copy-start(bf16[512,768]{1,0:T(8,128)(2,1)} %copy-done.8) | copy-start | bytes 2359300
  240.9 1.9 copy-start.14
  241.0 2.1 copy-start.13
  242.8 1.7 copy-start.23
  242.8 1.9 copy-start.15
  243.0 1.9 copy-start.20
  244.8 2.0 copy-start.26
  244.9 2.1 copy-start.7
  247.0 2.4 copy-start.21
  247.0 2.4 copy-start.4
  249.4 2.4 copy-start.22
  251.8 4.1 %copy-start.10 = (bf16[512,3072]{1,0:T(8,128)(2,1)S(1)}, bf16[512,3072]{1,0:T(8,128)(2,1)}, u32[]{:S(2)}) copy-start(bf16[512,3072]{1,0:T(8,128)(2,1)} %get-tuple-element.78) | copy-start | bytes 9437188
  251.8 4.1 %copy-start.19 = (bf16[512,768]{1,0:T(8,128)(2,1)S(1)}, bf16[512,768]{1,0:T(8,128)(2,1)}, u32[]{:S(2)}) copy-start(bf16[512,768]{1,0:T(8,128)(2,1)} %param.23) | copy-start | bytes 2359300

commit v3 on v2

v3 whole, which is shorter than its diff:
```python
import functools
import math

import jax, jax.numpy as jnp
from jax import lax
from jax.experimental import pallas as pl
from jax.experimental.pallas import tpu as pltpu
from jax.sharding import PartitionSpec as P

f32 = jnp.float32
bf16 = jnp.bfloat16
NT = (((1,), (1,)), ((), ()))
TN = (((0,), (0,)), ((), ()))


def dot(a, b, dims=(((1,), (0,)), ((), ()))):
    return lax.dot_general(a, b, dims, preferred_element_type=f32)


def lookup(row, index):
    shape = index.shape
    low = jnp.broadcast_to(row[:, :128], shape)
    high = jnp.broadcast_to(row[:, 128:], shape)
    inner = index & 127
    return jnp.where(
        index < 128,
        jnp.take_along_axis(low, inner, axis=1),
        jnp.take_along_axis(high, inner, axis=1),
    )


def forward_half(half, q_ref, k_ref, v_ref, table_ref, buckets_ref, segc_ref, segr_ref, attn_ref, p_ref):
    seq = q_ref.shape[0]
    even = lax.broadcasted_iota(jnp.int32, (1, 128), 1) < 64
    mine = even if half == 0 else jnp.logical_not(even)
    rows = 128
    row = table_ref[0, half : half + 1, :]
    k = k_ref[...]
    v = v_ref[...]

    def body(step, carry):
        at = pl.ds(pl.multiple_of(step * rows, rows), rows)
        q = jnp.where(mine, q_ref[at, :], jnp.zeros((), bf16))
        raw = dot(q, k, NT) * 0.125
        bias = jnp.concatenate(
            [lookup(row, buckets_ref[at, pl.ds(128 * j, 128)]) for j in range(seq // 128)], axis=1
        )
        same = segc_ref[at, :] == segr_ref[...]
        scores = jnp.where(same, raw + bias, -1e9)
        top = jnp.max(scores, axis=1, keepdims=True)
        expo = jnp.exp(scores - top)
        total = jnp.sum(expo, axis=1, keepdims=True)
        probs = (expo * (1.0 / total)).astype(bf16)
        p_ref[half, at, :] = probs
        out = dot(probs, v)
        if half == 0:
            attn_ref[at, :] = out
        else:
            attn_ref[at, :] = jnp.where(even, attn_ref[at, :], out)
        return carry

    lax.fori_loop(0, seq // rows, body, 0)


def forward_kernel(*refs):
    for half in range(2):
        forward_half(half, *refs)


def spread(steps, first, slots):
    plan = [[] for _ in range(slots)]
    plan[0] += first
    for i, step in enumerate(steps):
        plan[1 + i * (slots - 1) // len(steps)].append(step)
    return plan


def run_at(where, plan):
    for k, steps in enumerate(plan):
        if steps:

            @pl.when(where == k)
            def _():
                for step in steps:
                    step()


def forward_gather_kernel(count, pairs, *refs):
    ins, shards, outs = refs[:7], refs[7 : 7 + count], refs[7 + count : 9 + count]
    wholes = refs[9 + count : 9 + 2 * count]
    local_sem, send_sem, recv_sem = refs[9 + 2 * count :]
    place = Place()
    jobs = [
        Gather(place, shards[i], wholes[i], local_sem.at[i], send_sem.at[i], recv_sem.at[i])
        for i in range(count)
    ]
    plan = spread(gather_steps(jobs), [place.greet] + [job.begin for job in jobs], 2 * pairs)
    pair = pl.program_id(0)
    for half in range(2):
        run_at(pair, plan[half::2])
        forward_half(half, *ins, *outs)
    run_at(pair, [[]] * (pairs - 1) + [[job.finish for job in jobs] + [job.drain for job in jobs]])


def attention_forward(qkv, table_t, buckets, segments, shards=()):
    seq, width = qkv.shape[0], qkv.shape[1] // 3
    pairs = width // 128
    nb = table_t.shape[2]
    count = len(shards)
    kernel, scratch, params = forward_kernel, [], None
    if count:
        kernel = functools.partial(forward_gather_kernel, count, pairs)
        scratch = gather_scratch(count)
        params = pltpu.CompilerParams(collective_id=2, has_side_effects=True)
    attn, probs, *wholes = pl.pallas_call(
        kernel,
        grid=(pairs,),
        in_specs=[
            pl.BlockSpec((seq, 128), lambda i: (0, i)),
            pl.BlockSpec((seq, 128), lambda i: (0, pairs + i)),
            pl.BlockSpec((seq, 128), lambda i: (0, 2 * pairs + i)),
            pl.BlockSpec((1, 2, nb), lambda i: (i, 0, 0)),
            pl.BlockSpec((seq, seq), lambda i: (0, 0)),
            pl.BlockSpec((seq, 1), lambda i: (0, 0)),
            pl.BlockSpec((1, seq), lambda i: (0, 0)),
        ]
        + [pl.BlockSpec(memory_space=pltpu.VMEM)] * count,
        out_specs=[
            pl.BlockSpec((seq, 128), lambda i: (0, i)),
            pl.BlockSpec((2, seq, seq), lambda i: (i, 0, 0)),
        ]
        + [pl.BlockSpec(memory_space=pl.ANY)] * count,
        out_shape=[
            jax.ShapeDtypeStruct((seq, width), f32),
            jax.ShapeDtypeStruct((2 * pairs, seq, seq), bf16),
        ]
        + [whole_shape(x) for x in shards],
        scratch_shapes=scratch,
        compiler_params=params,
        name="attention_forward",
    )(qkv, qkv, qkv, table_t, buckets, segments.reshape(seq, 1), segments.reshape(1, seq), *shards)
    return attn, probs, [w.reshape(32 * x.shape[0], x.shape[1]) for w, x in zip(wholes, shards)]


HIGH = 4


def backward_half(half, pair, q_ref, k_ref, v_ref, do_ref, attn_ref, p_ref, dq_ref, dk_ref, dv_ref, ds_ref, dst_ref):
    seq = q_ref.shape[0]
    even = lax.broadcasted_iota(jnp.int32, (1, 128), 1) < 64
    mine = even if half == 0 else jnp.logical_not(even)
    rows = 128
    chunks = seq // 128
    k = k_ref[...]
    v = v_ref[...]
    head = pair * 2 + half

    def body(step, carry):
        at = pl.ds(pl.multiple_of(step * rows, rows), rows)
        do = jnp.where(mine, do_ref[at, :], jnp.zeros((), bf16))
        probs = p_ref[half, at, :]
        delta = jnp.sum(do.astype(f32) * attn_ref[at, :], axis=1, keepdims=True)
        ds = probs.astype(f32) * (dot(do, v, NT) - delta)
        for j in range(chunks):
            ds_ref[j, pl.ds(step * rows * 16 + head, rows, stride=16), :] = ds[:, 128 * j : 128 * j + 128]
        ds = ds.astype(bf16)
        dst_ref[at, :] = ds
        dq = dot(ds, k) * 0.125
        if half == 0:
            dq_ref[at, :] = dq.astype(bf16)
        else:
            dq_ref[at, :] = jnp.where(even, dq_ref[at, :], dq.astype(bf16))
        return carry

    lax.fori_loop(0, seq // rows, body, 0)
    dk = (dot(dst_ref[...], q_ref[...], TN) * 0.125).astype(bf16)
    dv = dot(p_ref[half], do_ref[...], TN).astype(bf16)
    if half == 0:
        dk_ref[...] = dk
        dv_ref[...] = dv
    else:
        dk_ref[...] = jnp.where(even, dk_ref[...], dk)
        dv_ref[...] = jnp.where(even, dv_ref[...], dv)


def histogram(part, parts, buckets_ref, ds_ref, acc_ref):
    seq = buckets_ref.shape[0]
    chunks = seq // 128
    group = 8
    low = acc_ref.shape[1]

    def body(step, carry):
        base = pl.multiple_of(step * group, group)
        ids = buckets_ref[pl.ds(base, group), :]
        left, right = [], []
        for r in range(group):
            at = pl.ds(pl.multiple_of((base + r) * 16, 16), 16)
            d = jnp.concatenate([ds_ref[j, at, :] for j in range(chunks)], axis=1)
            idr = ids[r : r + 1, :]
            top = idr // low
            left.append(jnp.concatenate([jnp.where(top == b, d, 0.0) for b in range(HIGH)], axis=0).astype(bf16))
            which = lax.broadcasted_iota(jnp.int32, (low, seq), 0)
            right.append(jnp.where(which == (idr & (low - 1)), 1.0, 0.0).astype(bf16))
        acc_ref[...] += dot(jnp.concatenate(left, axis=1), jnp.concatenate(right, axis=1), NT)
        return carry

    steps = seq // group // parts
    lax.fori_loop(part * steps, (part + 1) * steps, body, 0)


PARTS = 4


def backward_kernel(count, *refs):
    ins, buckets_ref, parts = refs[:6], refs[6], refs[7 : 7 + count]
    outs, hist_ref, sums = refs[7 + count : 10 + count], refs[10 + count], refs[11 + count : 11 + 2 * count]
    ds_ref, dst_ref, acc_ref, *scratch = refs[11 + 2 * count :]
    pair = pl.program_id(0)
    pairs = 6 if count else None
    if count:
        place = Place()
        jobs = [Reduce(place, parts[i], sums[i], scratch[9 * i : 9 * i + 9]) for i in range(count)]
        plan = spread(reduce_steps(jobs), [place.greet] + [job.begin for job in jobs], 2 * pairs + PARTS)

    @pl.when(pair == 0)
    def _():
        acc_ref[...] = jnp.zeros_like(acc_ref)

    for half in range(2):
        if count:
            run_at(pair, plan[half : 2 * pairs : 2])
        backward_half(half, pair, *ins, *outs, ds_ref, dst_ref)

    @pl.when(pair == pl.num_programs(0) - 1)
    def _():
        for part in range(PARTS):
            if count:
                for step in plan[2 * pairs + part]:
                    step()
            histogram(part, PARTS, buckets_ref, ds_ref, acc_ref)
        hist_ref[...] = acc_ref[...]
        if count:
            for job in jobs:
                job.finish()
            for job in jobs:
                job.drain()


def attention_backward(qkv, d_attn, attn, p, buckets, nb, parts=()):
    seq, width = d_attn.shape
    pairs = width // 128
    low = nb // HIGH
    count = len(parts)
    narrow = lambda first: pl.BlockSpec((seq, 128), lambda i: (0, first + i))
    scratch, params, shapes = [], None, []
    if count:
        shapes = [(x.shape[0] // 32, x.shape[1]) for x in parts]
        for x, shape in zip(parts, shapes):
            scratch += Reduce.scratch(shape, x.dtype)
        parts = [x.reshape((4, 2, 2, 2) + shape) for x, shape in zip(parts, shapes)]
        params = pltpu.CompilerParams(collective_id=3, has_side_effects=True, vmem_limit_bytes=63 * 2**20)
    dq, dk, dv, hist, *sums = pl.pallas_call(
        functools.partial(backward_kernel, count),
        grid=(pairs,),
        in_specs=[
            narrow(0), narrow(pairs), narrow(2 * pairs), narrow(0), narrow(0),
            pl.BlockSpec((2, seq, seq), lambda i: (i, 0, 0)),
            pl.BlockSpec((seq, seq), lambda i: (0, 0), pipeline_mode=pl.Buffered(1)),
        ]
        + [pl.BlockSpec(memory_space=pltpu.VMEM)] * count,
        out_specs=[narrow(0), narrow(0), narrow(0), pl.BlockSpec((HIGH * 16, low), lambda i: (0, 0))]
        + [pl.BlockSpec(memory_space=pltpu.VMEM)] * count,
        out_shape=[jax.ShapeDtypeStruct((seq, width), bf16)] * 3
        + [jax.ShapeDtypeStruct((HIGH * 16, low), f32)]
        + [jax.ShapeDtypeStruct(shape, f32) for shape in shapes],
        scratch_shapes=[
            pltpu.VMEM((seq // 128, seq * 16, 128), f32),
            pltpu.VMEM((seq, seq), bf16),
            pltpu.VMEM((HIGH * 16, low), f32),
        ]
        + scratch,
        compiler_params=params,
        name="attention_backward",
    )(qkv, qkv, qkv, d_attn, attn, p, buckets, *parts)
    return dq, dk, dv, hist, sums


def table_gradient(hist, heads):
    high, low = HIGH, hist.shape[1]
    return hist.reshape(high, 16, low)[:, :heads].transpose(0, 2, 1).reshape(high * low, heads)

MESH = pl.DeviceIdType.MESH


class Place:
    def __init__(self):
        wide, narrow = lax.axis_index("wide"), lax.axis_index("narrow")
        self.z, self.x = wide // 2, wide % 2
        self.y, self.c = narrow // 2, narrow % 2

    def device(self, z=None, x=None, y=None, c=None):
        z = self.z if z is None else z
        x = self.x if x is None else x
        y = self.y if y is None else y
        c = self.c if c is None else c
        return (z * 2 + x, y * 2 + c)

    def peers(self):
        out = [self.device(z=(self.z + d) % 4) for d in (1, 2, 3)]
        return out + [self.device(x=1 - self.x), self.device(y=1 - self.y), self.device(c=1 - self.c)]

    def greet(self):
        barrier = pltpu.get_barrier_semaphore()
        for peer in self.peers():
            pl.semaphore_signal(barrier, inc=1, device_id=peer, device_id_type=MESH)
        pl.semaphore_wait(barrier, 6)


def send(src, dst, send_sem, recv_sem, to):
    copy = pltpu.make_async_remote_copy(
        src_ref=src, dst_ref=dst, send_sem=send_sem, recv_sem=recv_sem, device_id=to, device_id_type=MESH
    )
    copy.start()
    return copy


class Gather:
    SLOTS = 35

    def __init__(self, place, shard, whole, local_sem, send_sem, recv_sem):
        self.p, self.shard, self.whole = place, shard, whole
        self.local_sem, self.send_sem, self.recv_sem = local_sem, send_sem, recv_sem
        self.width = shard.shape[-1]
        self.half = (self.width // 256) * 128

    def at(self, z, x, y, c, part=None):
        ref = self.whole.at[z, x, y, c]
        if part == 0:
            return ref.at[:, pl.ds(0, self.half)]
        if part == 1:
            return ref.at[:, pl.ds(self.half, self.width - self.half)]
        return ref

    def go(self, src, dst, slot, to):
        send(src, dst, self.send_sem.at[slot], self.recv_sem.at[slot], to)

    def arrived(self, dst, slot):
        pltpu.make_async_copy(dst, dst, self.recv_sem.at[slot]).wait()

    def begin(self):
        p = self.p
        mine = self.at(p.z, p.x, p.y, p.c)
        pltpu.make_async_copy(self.shard, mine, self.local_sem).start()
        for d in (1, 2, 3):
            self.go(self.shard, mine, d - 1, p.device(z=(p.z + d) % 4))
        self.go(self.shard, mine, 3, p.device(x=1 - p.x))
        self.go(self.shard, mine, 7, p.device(y=1 - p.y))
        self.go(self.shard, mine, 19, p.device(c=1 - p.c))

    def line(self, d):
        p = self.p
        ref = self.at((p.z + 4 - d) % 4, p.x, p.y, p.c)
        self.arrived(ref, d - 1)
        self.go(ref, ref, 3 + d, p.device(x=1 - p.x))
        self.go(ref, ref, 7 + d, p.device(y=1 - p.y))
        self.go(ref, ref, 19 + d, p.device(c=1 - p.c))

    def cross(self, d):
        p = self.p
        z = (p.z + 4 - d) % 4
        ref = self.at(z, 1 - p.x, p.y, p.c)
        self.arrived(ref, 3 + d)
        if self.half:
            part = self.at(z, 1 - p.x, p.y, p.c, 0)
            self.go(part, part, 11 + d, p.device(y=1 - p.y))
        self.go(ref, ref, 23 + d, p.device(c=1 - p.c))
        ref = self.at(z, p.x, 1 - p.y, p.c)
        self.arrived(ref, 7 + d)
        part = self.at(z, p.x, 1 - p.y, p.c, 1)
        self.go(part, part, 15 + d, p.device(x=1 - p.x))
        self.go(ref, ref, 27 + d, p.device(c=1 - p.c))

    def corner(self, d):
        p = self.p
        z = (p.z + 4 - d) % 4
        if self.half:
            self.arrived(self.at(z, 1 - p.x, 1 - p.y, p.c, 0), 11 + d)
        self.arrived(self.at(z, 1 - p.x, 1 - p.y, p.c, 1), 15 + d)
        ref = self.at(z, 1 - p.x, 1 - p.y, p.c)
        self.go(ref, ref, 31 + d, p.device(c=1 - p.c))

    def finish(self):
        p = self.p
        other = 1 - p.c
        for d in range(4):
            z = (p.z + 4 - d) % 4
            self.arrived(self.at(z, p.x, p.y, other), 19 + d)
            self.arrived(self.at(z, 1 - p.x, p.y, other), 23 + d)
            self.arrived(self.at(z, p.x, 1 - p.y, other), 27 + d)
            self.arrived(self.at(z, 1 - p.x, 1 - p.y, other), 31 + d)

    def drain(self):
        pltpu.make_async_copy(self.shard, self.at(0, 0, 0, 0), self.local_sem).wait()
        for slot in range(self.SLOTS):
            part = 0 if 11 <= slot < 15 else 1 if 15 <= slot < 19 else None
            if part == 0 and not self.half:
                continue
            ref = self.at(0, 0, 0, 0, part)
            pltpu.make_async_copy(ref, ref, self.send_sem.at[slot]).wait()


def gather_steps(jobs):
    stages = []
    for i, job in enumerate(jobs):
        line = [functools.partial(job.line, d) for d in (1, 2, 3)]
        cross = [functools.partial(job.cross, d) for d in range(4)]
        corner = [functools.partial(job.corner, d) for d in range(4)]
        stages += [((i, 0, k), f) for k, f in enumerate(line)]
        stages += [((i + 1, 1, k), f) for k, f in enumerate(cross)]
        stages += [((i + 2, 2, k), f) for k, f in enumerate(corner)]
    return [f for _, f in sorted(stages, key=lambda pair: pair[0])]


def gather_scratch(count):
    return [
        pltpu.SemaphoreType.DMA((count,)),
        pltpu.SemaphoreType.DMA((count, Gather.SLOTS)),
        pltpu.SemaphoreType.DMA((count, Gather.SLOTS)),
    ]


def whole_shape(shard):
    return jax.ShapeDtypeStruct((4, 2, 2, 2) + shard.shape, shard.dtype)


def gather_first_kernel(count, *refs):
    vectors, table, shard = refs[:count], refs[count], refs[count + 1]
    whole, whole_tile, tile, local_sem, send_sem, recv_sem = refs[count + 2 :]
    tile[...] = jnp.zeros_like(tile)
    for i, v in enumerate(vectors):
        tile[i : i + 1, : v.shape[1]] = v[...].astype(f32)
    tile[16:24, : table.shape[1]] = table[...].astype(f32)
    place = Place()
    place.greet()
    pairs = [(shard, whole), (tile, whole_tile)]
    jobs = [Gather(place, s, w, local_sem.at[i], send_sem.at[i], recv_sem.at[i]) for i, (s, w) in enumerate(pairs)]
    for job in jobs:
        job.begin()
    for step in gather_steps(jobs):
        step()
    for job in jobs:
        job.finish()
    for job in jobs:
        job.drain()


def gather_first(shard, vectors, table):
    tile = jax.ShapeDtypeStruct((24, 128), f32)
    whole, tiles = pl.pallas_call(
        functools.partial(gather_first_kernel, len(vectors)),
        in_specs=[pl.BlockSpec(memory_space=pltpu.VMEM)] * (len(vectors) + 2),
        out_specs=[pl.BlockSpec(memory_space=pl.ANY)] * 2,
        out_shape=[whole_shape(shard), whole_shape(tile)],
        scratch_shapes=[pltpu.VMEM((24, 128), f32)] + gather_scratch(2),
        compiler_params=pltpu.CompilerParams(collective_id=0, has_side_effects=True),
        name="gather_first",
    )(*[v[None, :] for v in vectors], table, shard)
    return whole.reshape(32 * shard.shape[0], shard.shape[1]), tiles.reshape(32, 24, 128)


class Reduce:
    SLOTS = 12

    @staticmethod
    def scratch(shape, dtype):
        rows, width = shape
        half = (width // 256) * 128
        four = lambda w: pltpu.VMEM((4, rows, w), dtype)
        return [
            pltpu.VMEM((4, 4, rows, width), dtype),
            pltpu.VMEM((4, 4, rows, width), dtype),
            four(max(half, 128)), four(width - half), four(width), four(width),
            pltpu.VMEM((3, rows, width), dtype),
            pltpu.SemaphoreType.DMA((Reduce.SLOTS,)),
            pltpu.SemaphoreType.DMA((Reduce.SLOTS,)),
        ]

    def __init__(self, place, parts, out, scratch):
        self.p, self.parts, self.out = place, parts, out
        (self.other, self.ready, self.by_y, self.by_x, self.from_x, self.from_y, self.from_z,
         self.send_sem, self.recv_sem) = scratch
        width = out.shape[-1]
        self.half, self.width = (width // 256) * 128, width

    def go(self, src, dst, slot, to):
        send(src, dst, self.send_sem.at[slot], self.recv_sem.at[slot], to)

    def arrived(self, dst, slot):
        pltpu.make_async_copy(dst, dst, self.recv_sem.at[slot]).wait()

    def spots(self):
        p = self.p
        return [(1 - p.x, 1 - p.y), (1 - p.x, p.y), (p.x, 1 - p.y), (p.x, p.y)]

    def begin(self):
        p = self.p
        for i, (x, y) in enumerate(self.spots()):
            self.go(self.parts.at[:, x, y, 1 - p.c], self.other.at[i], i, p.device(c=1 - p.c))

    def pair(self, i, z):
        x, y = self.spots()[i]
        return self.parts[z, x, y, self.p.c].astype(f32) + self.other[i, z].astype(f32)

    def corner(self):
        p, half = self.p, self.half
        self.arrived(self.other.at[0], 0)

        @pl.loop(0, 4)
        def _(z):
            self.ready[0, z] = self.pair(0, z).astype(self.ready.dtype)

        if half:
            self.go(self.ready.at[0, :, :, pl.ds(0, half)], self.by_y, 4, p.device(y=1 - p.y))
        self.go(self.ready.at[0, :, :, pl.ds(half, self.width - half)], self.by_x, 5, p.device(x=1 - p.x))

    def cross(self):
        p, half = self.p, self.half
        self.arrived(self.other.at[1], 1)
        if half:
            self.arrived(self.by_y, 4)

        @pl.loop(0, 4)
        def _(z):
            total = self.pair(1, z)
            if half:
                total = jnp.concatenate([total[:, :half] + self.by_y[z].astype(f32), total[:, half:]], axis=1)
            self.ready[1, z] = total.astype(self.ready.dtype)

        self.go(self.ready.at[1], self.from_x, 6, p.device(x=1 - p.x))

    def cross_y(self):
        p, half = self.p, self.half
        self.arrived(self.other.at[2], 2)
        self.arrived(self.by_x, 5)

        @pl.loop(0, 4)
        def _(z):
            total = self.pair(2, z)
            right = total[:, half:] + self.by_x[z].astype(f32)
            total = jnp.concatenate([total[:, :half], right], axis=1) if half else right
            self.ready[2, z] = total.astype(self.ready.dtype)

        self.go(self.ready.at[2], self.from_y, 7, p.device(y=1 - p.y))

    def line(self):
        p = self.p
        self.arrived(self.other.at[3], 3)
        self.arrived(self.from_x, 6)
        self.arrived(self.from_y, 7)
        for d in (1, 2, 3):
            z = (p.z + d) % 4
            total = self.pair(3, z) + self.from_x[z].astype(f32) + self.from_y[z].astype(f32)
            self.ready[3, z] = total.astype(self.ready.dtype)
            self.go(self.ready.at[3, z], self.from_z.at[d - 1], 7 + d, p.device(z=z))

    def finish(self):
        p = self.p
        for d in (1, 2, 3):
            self.arrived(self.from_z.at[d - 1], 7 + d)
        total = self.pair(3, p.z) + self.from_x[p.z].astype(f32) + self.from_y[p.z].astype(f32)
        for d in (1, 2, 3):
            total = total + self.from_z[d - 1].astype(f32)
        self.out[...] = total

    def drain(self):
        for slot in range(11):
            if slot == 4 and not self.half:
                continue
            ref = (self.by_y if slot == 4 else self.by_x if slot == 5 else
                   self.other.at[0] if slot < 8 else self.from_z.at[0])
            pltpu.make_async_copy(ref, ref, self.send_sem.at[slot]).wait()


class Everywhere:
    @staticmethod
    def scratch(shape):
        return [pltpu.VMEM((3,) + shape, f32), pltpu.VMEM((6,) + shape, f32),
                pltpu.SemaphoreType.DMA((6,)), pltpu.SemaphoreType.DMA((6,))]

    def __init__(self, place, block, out, scratch):
        self.p, self.block, self.out = place, block, out
        self.mine, self.got, self.send_sem, self.recv_sem = scratch

    def go(self, src, slot, to):
        send(src, self.got.at[slot], self.send_sem.at[slot], self.recv_sem.at[slot], to)

    def arrived(self, slot):
        dst = self.got.at[slot]
        pltpu.make_async_copy(dst, dst, self.recv_sem.at[slot]).wait()

    def begin(self):
        self.go(self.block, 0, self.p.device(c=1 - self.p.c))

    def corner(self):
        self.arrived(0)
        self.mine[0] = self.block[...] + self.got[0]
        self.go(self.mine.at[0], 1, self.p.device(x=1 - self.p.x))

    def cross(self):
        self.arrived(1)
        self.mine[1] = self.mine[0] + self.got[1]
        self.go(self.mine.at[1], 2, self.p.device(y=1 - self.p.y))

    def cross_y(self):
        pass

    def line(self):
        p = self.p
        self.arrived(2)
        self.mine[2] = self.mine[1] + self.got[2]
        for d in (1, 2, 3):
            self.go(self.mine.at[2], 2 + d, p.device(z=(p.z + d) % 4))

    def finish(self):
        p = self.p
        for d in (1, 2, 3):
            self.arrived(2 + d)
        total = None
        for z in range(4):
            term = jnp.where(p.z == z, self.mine[2], 0.0)
            for d in (1, 2, 3):
                term = term + jnp.where((p.z + 4 - d) % 4 == z, self.got[2 + d], 0.0)
            total = term if total is None else total + term
        self.out[...] = total

    def drain(self):
        for slot in range(6):
            ref = self.got.at[slot]
            pltpu.make_async_copy(ref, ref, self.send_sem.at[slot]).wait()


def reduce_steps(jobs):
    stages = []
    for i, job in enumerate(jobs):
        stages += [((i, 0), job.corner), ((i + 1, 1), job.cross), ((i + 1, 2), job.cross_y), ((i + 2, 3), job.line)]
    return [f for _, f in sorted(stages, key=lambda pair: pair[0])]


def reduce_kernel(count, extra, *refs):
    total = count + extra
    parts, outs, scratch = refs[:total], refs[total : 2 * total], refs[2 * total :]
    place = Place()
    place.greet()
    jobs = [Reduce(place, parts[i], outs[i], scratch[9 * i : 9 * i + 9]) for i in range(count)]
    if extra:
        jobs.append(Everywhere(place, parts[count], outs[count], scratch[9 * count :]))
    for job in jobs:
        job.begin()
    for step in reduce_steps(jobs):
        step()
    for job in jobs:
        job.finish()
    for job in jobs:
        job.drain()


def reduce_all(parts, block, collective_id):
    shapes = [(p.shape[0] // 32, p.shape[1]) for p in parts]
    given = [p.reshape((4, 2, 2, 2) + s) for p, s in zip(parts, shapes)]
    outs = [jax.ShapeDtypeStruct(s, f32) for s in shapes]
    scratch = []
    for p, s in zip(parts, shapes):
        scratch += Reduce.scratch(s, p.dtype)
    extra = block is not None
    if extra:
        given.append(block)
        outs.append(jax.ShapeDtypeStruct(block.shape, f32))
        scratch += Everywhere.scratch(block.shape)
    return pl.pallas_call(
        functools.partial(reduce_kernel, len(parts), int(extra)),
        in_specs=[pl.BlockSpec(memory_space=pltpu.VMEM)] * len(given),
        out_specs=[pl.BlockSpec(memory_space=pltpu.VMEM)] * len(outs),
        out_shape=outs,
        scratch_shapes=scratch,
        compiler_params=pltpu.CompilerParams(
            collective_id=collective_id, has_side_effects=True, vmem_limit_bytes=60 * 2**20
        ),
        name="reduce_all",
    )(*given)


def finish_kernel(count, sizes, *refs):
    tile, sums, outs = refs[0], refs[1 : 1 + count], refs[1 + count :]
    for src, dst in zip(sums, outs):
        dst[...] = src[...]
    for i, size in enumerate(sizes):
        outs[count + i][...] = tile[i : i + 1, :size]
    table = outs[count + len(sizes)]
    table[...] = tile[16:24, : table.shape[1]]


def finish(tile, sums, sizes, columns):
    outs = [jax.ShapeDtypeStruct(a.shape, f32) for a in sums]
    outs += [jax.ShapeDtypeStruct((1, n), f32) for n in sizes] + [jax.ShapeDtypeStruct((8, columns), f32)]
    out = pl.pallas_call(
        functools.partial(finish_kernel, len(sums), sizes),
        in_specs=[pl.BlockSpec(memory_space=pltpu.VMEM)] * (1 + len(sums)),
        out_specs=[pl.BlockSpec(memory_space=pltpu.VMEM)] * len(outs),
        out_shape=outs,
        name="finish",
    )(tile, *sums)
    n = len(sums)
    return out[:n], [v.reshape(-1) for v in out[n : n + len(sizes)]], out[-1]

AXES = ("wide", "narrow")


def standardize(v):
    centred = v - jnp.mean(v, axis=-1, keepdims=True)
    inverse = lax.rsqrt(jnp.mean(centred * centred, axis=-1, keepdims=True) + 1e-05)
    return centred * inverse, inverse


def norm_back(grad, normed, inverse, gain):
    scaled = grad * gain
    return inverse * (
        scaled
        - jnp.mean(scaled, axis=-1, keepdims=True)
        - normed * jnp.mean(scaled * normed, axis=-1, keepdims=True)
    )


def lanes(x):
    return jnp.pad(x, ((0, 0), (0, 0), (0, 128 - x.shape[2])))


def pack_tiles(vectors, table, devices):
    rows = [lanes(v.reshape(devices, 1, -1)) for v in vectors]
    rows.append(jnp.zeros((devices, 16 - len(vectors), 128), f32))
    rows.append(lanes(table.reshape(devices, 8, -1)))
    return jnp.concatenate(rows, axis=1)


def unpack_tiles(tiles, sizes, columns):
    vectors = [tiles[:, i, :size].reshape(-1) for i, size in enumerate(sizes)]
    return vectors, tiles[:, 16:24, :columns].reshape(-1, columns)


def whole_of(x):
    return lax.all_gather(x, AXES, axis=0, tiled=True)


def share_of(x):
    return lax.psum_scatter(x, AXES, scatter_dimension=0, tiled=True)


def local(devices, direct, tokens, cotangent, segments, buckets, norm1_gain, norm1_bias, qkv_weight, qv_bias,
          head_scale, rel_table, out_weight, out_bias, post_gain, post_bias, norm2_gain, norm2_bias,
          fc1_weight, fc1_bias, inner_gain, inner_bias, fc2_weight, fc2_bias):
    seq, width = tokens.shape
    heads = head_scale.shape[0]
    size = width // heads
    small = (norm1_gain, norm1_bias, out_bias, post_gain, post_bias, norm2_gain, norm2_bias, fc2_bias,
             qv_bias, fc1_bias, inner_gain, inner_bias)
    sizes = [v.shape[0] for v in small]
    nb = rel_table.shape[0] * devices
    held = bf16 if direct else f32
    late = (out_weight, fc1_weight, fc2_weight)
    if direct:
        w_qkv, tiles = gather_first(qkv_weight, small, rel_table)
        vectors, table = unpack_tiles(tiles, sizes, heads)
    else:
        w_qkv = whole_of(qkv_weight)
        vectors = [whole_of(v).astype(f32) for v in small]
        table = whole_of(rel_table).astype(f32)
        w_out, w_first, w_second = [whole_of(w) for w in late]
        late = ()
    (gain_one, bias_one, bias_out, gain_post, bias_post, gain_two, bias_two, bias_second,
     bias_qv, bias_first, gain_inner, bias_inner) = vectors
    table_t = table.T.reshape(heads // 2, 2, nb)
    scale = jnp.repeat(head_scale.astype(f32), size)[None, :]

    inputs = tokens.astype(f32)
    hat_one, inv_one = standardize(inputs)
    h_one = (hat_one * gain_one + bias_one).astype(bf16)
    shift = jnp.concatenate([bias_qv[:width], jnp.zeros((width,), f32), bias_qv[width:]])
    qkv = (dot(h_one, w_qkv) + shift).astype(bf16)
    attn, probs, wholes = attention_forward(qkv, table_t, buckets, segments, late)
    if direct:
        w_out, w_first, w_second = wholes
    scaled = (attn * scale).astype(bf16)
    mixed = dot(scaled, w_out) + bias_out
    hat_post, inv_post = standardize(mixed)
    first = inputs + hat_post * gain_post + bias_post
    hat_two, inv_two = standardize(first)
    h_two = (hat_two * gain_two + bias_two).astype(bf16)
    inner = dot(h_two, w_first) + bias_first
    cdf = 0.5 * (1.0 + lax.erf(inner * (1.0 / math.sqrt(2.0))))
    hat_inner, inv_inner = standardize(inner * cdf)
    hidden = (hat_inner * gain_inner + bias_inner).astype(bf16)
    output = (first + (dot(hidden, w_second) + bias_second)).astype(bf16)

    grad_out = cotangent.astype(f32)
    g_second = dot(hidden, cotangent, TN).astype(held)
    g_second_bias = jnp.sum(grad_out, axis=0)
    d_hidden = dot(cotangent, w_second, NT)
    g_inner_gain = jnp.sum(d_hidden * hat_inner, axis=0)
    g_inner_bias = jnp.sum(d_hidden, axis=0)
    d_gelu = norm_back(d_hidden, hat_inner, inv_inner, gain_inner)
    pdf = jnp.exp(-0.5 * inner * inner) * (1.0 / math.sqrt(2.0 * math.pi))
    d_inner = (d_gelu * (cdf + inner * pdf)).astype(bf16)
    g_first_bias = jnp.sum(d_inner.astype(f32), axis=0)
    g_first = dot(h_two, d_inner, TN).astype(held)
    d_two = dot(d_inner, w_first, NT)
    g_two_gain = jnp.sum(d_two * hat_two, axis=0)
    g_two_bias = jnp.sum(d_two, axis=0)
    d_first = grad_out + norm_back(d_two, hat_two, inv_two, gain_two)
    g_post_gain = jnp.sum(d_first * hat_post, axis=0)
    g_post_bias = jnp.sum(d_first, axis=0)
    d_mixed = norm_back(d_first, hat_post, inv_post, gain_post).astype(bf16)
    g_out_bias = jnp.sum(d_mixed.astype(f32), axis=0)
    g_out = dot(scaled, d_mixed, TN).astype(held)
    d_scaled = dot(d_mixed, w_out, NT)
    g_scale = jnp.sum(jnp.sum(d_scaled * attn, axis=0).reshape(heads, size), axis=1)
    d_attn = (d_scaled * scale).astype(bf16)
    early = (g_second, g_first, g_out)
    dq, dk, dv, hist, sums = attention_backward(
        qkv, d_attn, attn, probs, buckets, nb, early if direct else ())
    g_table = table_gradient(hist, heads)
    dqkv = jnp.concatenate([dq, dk, dv], axis=1)
    g_qv = jnp.concatenate([jnp.sum(dq.astype(f32), axis=0), jnp.sum(dv.astype(f32), axis=0)])
    g_qkv = dot(h_one, dqkv, TN).astype(held)
    d_one = dot(dqkv, w_qkv, NT)
    g_one_gain = jnp.sum(d_one * hat_one, axis=0)
    g_one_bias = jnp.sum(d_one, axis=0)
    grad_tokens = (d_first + norm_back(d_one, hat_one, inv_one, gain_one)).astype(bf16)

    grads = (g_one_gain, g_one_bias, g_out_bias, g_post_gain, g_post_bias, g_two_gain, g_two_bias,
             g_second_bias, g_qv, g_first_bias, g_inner_gain, g_inner_bias)
    if direct:
        block = jnp.pad(g_scale[None, :], ((0, 7), (0, 128 - heads)))
        tiles = pack_tiles(grads, g_table, devices).reshape(devices * 24, 128)
        g_qkv, tile, block = reduce_all([g_qkv, tiles], block, 1)
        g_scale = block[0, :heads]
        (g_second, g_first, g_out, g_qkv), grads, g_table = finish(tile, [*sums, g_qkv], sizes, heads)
    else:
        g_second, g_first, g_out, g_qkv = [share_of(g) for g in (*early, g_qkv)]
        grads = [share_of(g) for g in grads]
        g_table = share_of(g_table)
        g_scale = lax.psum(g_scale, AXES)
    (g_one_gain, g_one_bias, g_out_bias, g_post_gain, g_post_bias, g_two_gain, g_two_bias,
     g_second_bias, g_qv, g_first_bias, g_inner_gain, g_inner_bias) = grads
    return (output, grad_tokens, g_one_gain, g_one_bias, g_qkv, g_qv, g_scale, g_table, g_out, g_out_bias,
            g_post_gain, g_post_bias, g_two_gain, g_two_bias, g_first, g_first_bias, g_inner_gain,
            g_inner_bias, g_second, g_second_bias)


def solution(mesh):
    devices = mesh.shape["wide"] * mesh.shape["narrow"]
    direct = (mesh.shape["wide"], mesh.shape["narrow"]) == (8, 4)
    split, line, whole = P(AXES, None), P(AXES), P()
    return jax.shard_map(
        functools.partial(local, devices, direct),
        mesh=mesh,
        in_specs=(split, split, split, whole, line, line, split, line, whole, split, split, line, line,
                  line, line, line, split, line, line, line, split, line),
        out_specs=(split, split, line, line, split, line, whole, split, split, line, line, line, line,
                   line, split, line, line, line, split, line),
        check_vma=False,
    )
```

time: 362 us -> 318 us (0.88)
  Pallas kernels: 248 us -> 206 us
  local copies, waits for them, and re-layouts: 34.6 us -> 17.8 us
  matrix products: 52.7 us -> 63.4 us
    pallas_call x1, Pallas kernels: 88.1 us -> 37.1 us  [reduce_all(): pl.pallas_call(functools.partial(reduce_kernel, len(parts), int(extra)),...]
    dot_general x12, matrix products: 52.7 us -> 63.4 us  [dot(): return lax.dot_general(a, b, dims, preferred_element_type=f32)]
    unnamed x68 -> x60, local copies, waits for them, and re-layouts: 14.5 us -> 4.63 us
    pallas_call x3 -> x4, Pallas kernels: 159 us -> 169 us  [the longest x1 69.5 us: attention_backward(): pl.pallas_call(functools.partial(backward_kernel, count), grid=(pairs,),...]
    concatenate x2 -> x1, local copies, waits for them, and re-layouts: 8.22 us -> 2.28 us  [pack_tiles(): return jnp.concatenate(rows, axis=1)]
    reshape x18 -> x14, local copies, waits for them, and re-layouts: 6.46 us -> 2.52 us  [the longest x2 0.99 us: unpack_tiles(): return (vectors, tiles[:, 16:24, :columns].reshape(-1, columns))]
where the time goes in v3:
time: 318 us; the launch traced here: 314 us
  Pallas kernels  206 us (65%)
  matrix products  63.4 us (20%)
  other arithmetic  25.4 us (8%)
  local copies, waits for them, and re-layouts  17.8 us (6%)
    pallas_call x1, Pallas kernels, attention_backward(): pl.pallas_call(functools.partial(backward_kernel, count), grid=(pairs,),...  69.5 us
    pallas_call x1, Pallas kernels, attention_forward(): pl.pallas_call(kernel, grid=(pairs,), in_specs=[pl.BlockSpec((seq, 128),...  66.7 us
    dot_general x12, matrix products, dot(): return lax.dot_general(a, b, dims, preferred_element_type=f32)  63.4 us
    pallas_call x1, Pallas kernels, reduce_all(): pl.pallas_call(functools.partial(reduce_kernel, len(parts), int(extra)),...  37.1 us
    pallas_call x1, Pallas kernels, gather_first(): pl.pallas_call(functools.partial(gather_first_kernel, len(vectors)), in_s...  30.3 us
    reduce_sum x1, other arithmetic, local(): g_first_bias = jnp.sum(d_inner.astype(f32), axis=0)  9.17 us

profile of v3, /device:TPU:0, one launch (start us, length us, event | category | flops | bytes accessed | tf_op | source)
XLA Modules:
  0.0 314.0 jit_solution(11940695887642474829)
XLA Ops:
  0.7 30.3 %gather_first.1 = (bf16[4,2,2,2,24,2304]{5,4,3,2,1,0:T(8,128)(2,1)}, f32[4,2,2,2,24,128]{5,4,3,2,1,0:T(8,128)}) custom-call(bf16[1,24]{1,0:T(2,128)(2,1)} %bitcast.139, bf16[1,24]{1,0:T(2,128)(2,1)} %bitcast.140, bf16[1,24]{1,0:T(2,128)(2,1)} %bitcast.141, bf16[1,24]{1,0:T(2,128)(2,1)} %bitcast.142, bf16[1,24]{1,0:T(2,128)(2,1)} %bitcast.143, ...), custom_call_target="tpu_custom_call" | custom-call | tf_op jit(solution)/shard_map/gather_first/pallas_call | solution.py:459
  31.0 1.9 fusion.33
  32.9 0.1 mul.246
  33.0 0.1 add.160
  33.1 0.9 slice_reduce_fusion.4
  34.2 1.3 convert_reduce_fusion.1
  35.5 0.4 fusion.23
  35.9 5.5 %fusion.8.refs_0_.refs_1_.refs_2_ = bf16[512,2304]{1,0:T(8,128)(2,1)} fusion(bf16[768,2304]{1,0:T(8,128)(2,1)} %bitcast.155, f32[2304]{0:T(1024)S(1)} %pad_maximum_fusion, bf16[512,768]{1,0:T(8,128)(2,1)S(1)} %copy-done.6, f32[768]{0:T(1024)S(1)} %add.160, f32[768]{0:T(1024)S(1)} %mul.246, f32[512]{0:T(512)S(1)} %add_rsqrt_fusion.3, ...), kind=kOutput, calls=%fused_computation.22 | convolution fusion | flops 1816657920 | bytes 6704128 | tf_op jit(solution)/shard_map/dot_general | solution.py:17
  41.4 0.9 slice_bitcast_fusion
  42.4 0.6 reshape.252.refs_3_
  43.1 0.9 copy.66.refs_5_
  43.9 66.7 %attention_forward.1 = (f32[512,768]{1,0:T(8,128)}, bf16[12,512,512]{2,1,0:T(8,128)(2,1)}, bf16[4,2,2,2,24,768]{5,4,3,2,1,0:T(8,128)(2,1)}, bf16[4,2,2,2,24,3072...) custom-call(bf16[512,2304]{1,0:T(8,128)(2,1)} %fusion.8.refs_0_.refs_1_.refs_2_, ...), custom_call_target="tpu_custom_call" | custom-call | tf_op jit(solution)/shard_map/attention_forward/pallas_call | solution.py:115
  110.6 0.1 add.165
  110.8 2.6 fusion.34
  113.5 0.3 multiply_reduce_fusion.8
  113.8 0.1 mul.255
  113.9 0.1 add.170
  113.9 1.7 fusion.31
  115.6 0.3 multiply_reduce_fusion.7
  116.0 0.1 mul.261
  116.0 0.1 add.174
  116.1 1.2 slice_reduce_fusion.1
  117.5 6.9 %fusion.30 = (f32[512]{0:T(512)S(1)}, f32[512,3072]{1,0:T(8,128)S(1)}, f32[512,3072]{1,0:T(8,128)}) fusion(f32[3072]{0:T(1024)S(1)} %add.177, bf16[768,3072]{1,0:T(8,128)(2,1)} %bitcast.153, f32[512,768]{1,0:T(8,128)S(1)} %get-tuple-element.116, f32[768]{0:T(1024)S(1)} %add.174, f32[768]{0:T(1024)S(1)} %mul.261, f32[512]{0:T(512)S(1)} %add_rsqrt_fusion.1, ...), kind=kOutput, calls=%fused_computation.98 | convolution fusion | flops 2427321856 | bytes 18898944 | tf_op jit(solution)/shard_map/dot_general | solution.py:17
  124.3 0.8 multiply_reduce_fusion.1
  125.1 1.8 copy-done
  127.0 10.2 %fusion.6 = (f32[3072]{0:T(1024)S(1)}, f32[512]{0:T(512)S(1)}, f32[512]{0:T(512)S(1)}, f32[3072,512]{0,1:T(8,128)}) fusion(f32[512,3072]{1,0:T(8,128)} %copy-done, f32[512]{0:T(512)S(1)} %add_rsqrt_fusion, f32[512]{0:T(512)S(1)} %broadcast_multiply_fusion.2, f32[3072]{0:T(1024)S(1)} %mul.272, bf16[3072,768]{1,0:T(8,128)(2,1)} %bitcast.151, ...), kind=kOutput, calls=%fused_computation.9 | convolution fusion | flops 2428497920 | bytes 18120704 | tf_op jit(solution)/shard_map/dot_general | solution.py:17
  137.3 9.2 %convert_reduce_fusion = (f32[3072]{0:T(1024)S(1)}, bf16[512,3072]{1,0:T(8,128)(2,1)S(1)}, bf16[512,3072]{1,0:T(8,128)(2,1)S(1)}) fusion(f32[512,3072]{1,0:T(8,128)} %get-tuple-element.131, f32[3072]{0:T(1024)S(1)} %add.177, f32[512]{0:T(512)S(1)} %get-tuple-element.135, f32[512,3072]{1,0:T(8,128)} %copy-done, f32[512]{0:T(512)S(1)} %broadcast_multiply_fusion.2, ...), kind=kLoop, calls=%fused_computation.10 | loop fusion | flops 36172800 | bytes 25223168 | tf_op jit(solution)/shard_map/reduce_sum | solution.py:812
  146.5 6.5 %multiply_reduce_fusion.3 = (f32[768]{0:T(1024)S(1)}, f32[512]{0:T(512)S(1)}, f32[512]{0:T(512)S(1)}, f32[768]{0:T(1024)S(1)}, f32[512,768]{1,0:T(8,128)S(1)}) fusion(f32[512,768]{1,0:T(8,128)S(1)} %get-tuple-element.116, f32[512]{0:T(512)S(1)} %add_rsqrt_fusion.1, f32[512]{0:T(512)S(1)} %broadcast_multiply_fusion.9, f32[768]{0:T(1024)S(1)} %mul.261, ...), kind=kOutput, calls=%fused_computation.47 | convolution fusion | flops 2419455488 | bytes 11027456 | tf_op jit(solution)/shard_map/dot_general | solution.py:17
  153.0 1.7 multiply_reduce_fusion.4
  154.8 0.5 convert_reduce_fusion.5
  155.3 0.6 copy-done.3
  155.9 0.9 copy-done.5
  156.7 1.8 convolution_convert_fusion.3
  158.6 4.8 %convolution_convert_fusion.1 = bf16[768,3072]{1,0:T(8,128)(2,1)} fusion(bf16[512,3072]{1,0:T(8,128)(2,1)S(1)} %get-tuple-element.109, f32[512,768]{1,0:T(8,128)S(1)} %get-tuple-element.116, f32[768]{0:T(1024)S(1)} %add.174, f32[768]{0:T(1024)S(1)} %mul.261, f32[512]{0:T(512)S(1)} %add_rsqrt_fusion.1, f32[512]{0:T(512)S(1)} %broadcast_multiply_fusion.9), kind=kOutput, calls=%fused_computation.19 | convolution fusion | flops 2420244480 | bytes 9447424 | tf_op jit(solution)/shard_map/dot_general | solution.py:17
  163.4 2.3 multiply_reduce_fusion.2
  165.7 4.4 %convolution_convert_fusion.2 = bf16[3072,768]{1,0:T(8,128)(2,1)} fusion(bf16[512,3072]{1,0:T(8,128)(2,1)S(1)} %get-tuple-element.117, bf16[512,768]{1,0:T(8,128)(2,1)S(1)} %copy-done.12), kind=kOutput, calls=%fused_computation.20 | convolution fusion | flops 2418278400 | bytes 8650752 | tf_op jit(solution)/shard_map/dot_general | solution.py:17
  170.1 69.5 %attention_backward.1 = (bf16[512,768]{1,0:T(8,128)(2,1)}, bf16[512,768]{1,0:T(8,128)(2,1)}, bf16[512,768]{1,0:T(8,128)(2,1)}, f32[64,64]{1,0:T(8,128)}, f32[96,...) custom-call(bf16[512,2304]{1,0:T(8,128)(2,1)} %fusion.8.refs_0_.refs_1_.refs_2_, ...), custom_call_target="tpu_custom_call" | custom-call | tf_op jit(solution)/shard_map/attention_backward/pallas_call | solution.py:262
  239.6 1.4 convert_reduce_fusion.4
  241.0 0.1 concatenate.19
  241.1 1.3 convert_reduce_fusion.3
  242.4 0.1 concatenate.20
  242.7 1.0 copy-done.9
  243.7 0.2 copy-done.7
  243.9 6.8 %fusion.22 = (f32[768]{0:T(1024)S(1)}, f32[512]{0:T(512)}, f32[512]{0:T(512)}, f32[768]{0:T(1024)S(1)}, f32[512,768]{1,0:T(8,128)}) fusion(bf16[512,768]{1,0:T(8,128)(2,1)S(1)} %copy-done.7, f32[512]{0:T(512)S(1)} %add_rsqrt_fusion.3, f32[512]{0:T(512)S(1)} %broadcast_multiply_fusion.11, f32[768]{0:T(1024)S(1)} %mul.246, ...), kind=kOutput, calls=%fused_computation.41 | convolution fusion | flops 1815868928 | bytes 8274944 | tf_op jit(solution)/shard_map/dot_general | solution.py:17
  250.8 0.1 reshape.262
  250.9 0.1 copy.73
  251.1 0.1 reshape.263
  251.2 0.1 reshape.264
  251.4 0.1 reshape.268
  251.5 0.1 reshape.266
  251.6 0.1 reshape.267
  251.7 0.1 reshape.269
  251.8 3.2 %reduce_sum.307 = f32[3072]{0:T(1024)S(1)} reduce(f32[3072,512]{0,1:T(8,128)} %get-tuple-element.132, f32[]{:T(128)} %constant.29.clone.1), dimensions={1}, to_apply=%region_28.0 | reduce | flops 1569792 | bytes 6303748 | tf_op jit(solution)/shard_map/reduce_sum | solution.py:808
  255.0 0.1 reshape.271
  255.2 0.1 reshape.270
  255.3 2.3 concatenate.22
  257.6 4.7 %convolution_convert_fusion = bf16[768,2304]{1,0:T(8,128)(2,1)} fusion(bf16[512,2304]{1,0:T(8,128)(2,1)S(1)} %copy-done.15, bf16[512,768]{1,0:T(8,128)(2,1)S(1)} %copy-done.7, f32[768]{0:T(1024)} %copy-done.25, f32[768]{0:T(1024)} %copy-done.19, f32[512]{0:T(512)} %copy-done.23, f32[512]{0:T(512)} %copy-done.17), kind=kOutput, calls=%fused_computation.18 | convolution fusion | flops 1816068096 | bytes 6694912 | tf_op jit(solution)/shard_map/dot_general | solution.py:17
  262.4 0.1 reduce_sum.309
  262.5 0.6 pad.60.refs_2_
  263.1 37.1 %reduce_all.1 = (f32[24,2304]{1,0:T(8,128)}, f32[24,128]{1,0:T(8,128)}, f32[8,128]{1,0:T(8,128)}) custom-call(bf16[4,2,2,2,24,2304]{5,4,3,2,1,0:T(8,128)(2,1)} %bitcast.110, f32[4,2,2,2,24,128]{5,4,3,2,1,0:T(8,128)} %bitcast.111, f32[8,128]{1,0:T(8,128)} %pad.60.refs_2_), custom_call_target="tpu_custom_call" | custom-call | tf_op jit(solution)/shard_map/reduce_all/pallas_call | solution.py:679
  300.2 2.1 finish.1
  302.4 1.2 slice_bitcast_fusion.2
  303.6 3.2 %fusion.21 = bf16[512,768]{1,0:T(8,128)(2,1)} fusion(f32[512,768]{1,0:T(8,128)S(1)} %copy-done.4, bf16[512,768]{1,0:T(8,128)(2,1)} %param.22, f32[512,768]{1,0:T(8,128)} %get-tuple-element.134, f32[512]{0:T(512)S(1)} %broadcast_multiply_fusion.3, f32[512]{0:T(512)S(1)} %broadcast_multiply_fusion.4, f32[768]{0:T(1024)S(1)} %copy-done.20, ...), kind=kLoop, calls=%fused_computation.40 | loop fusion | flops 3932160 | bytes 4729856 | tf_op jit(solution)/shard_map/convert_element_type | solution.py:836
  306.9 6.8 %add_convert_fusion.1 = bf16[512,768]{1,0:T(8,128)(2,1)} fusion(f32[512,768]{1,0:T(8,128)S(1)} %copy-done.2, bf16[512,3072]{1,0:T(8,128)(2,1)} %copy-done.8, bf16[3072,768]{1,0:T(8,128)(2,1)} %bitcast.152, f32[768]{0:T(1024)S(1)} %add.186), kind=kOutput, calls=%fused_computation.54 | convolution fusion | flops 2417098752 | bytes 10226688 | tf_op jit(solution)/shard_map/dot_general | solution.py:17
  (100 shorter events, 1.4 us)
Async XLA Ops:
  0.7 34.8 %copy-start.6 = (bf16[512,768]{1,0:T(8,128)(2,1)S(1)}, bf16[512,768]{1,0:T(8,128)(2,1)}, u32[]{:S(2)}) copy-start(bf16[512,768]{1,0:T(8,128)(2,1)} %param.22) | copy-start | bytes 2359300
  33.0 210.7 %copy-start.19 = (f32[768]{0:T(1024)}, f32[768]{0:T(1024)S(1)}, u32[]{:S(2)}) copy-start(f32[768]{0:T(1024)S(1)} %mul.246) | copy-start | bytes 9220
  33.1 8.4 %copy-start.25 = (f32[768]{0:T(1024)}, f32[768]{0:T(1024)S(1)}, u32[]{:S(2)}) copy-start(f32[768]{0:T(1024)S(1)} %add.160) | copy-start | bytes 9220
  35.5 208.2 %copy-start.17 = (f32[512]{0:T(512)}, f32[512]{0:T(512)S(1)}, u32[]{:S(2)}) copy-start(f32[512]{0:T(512)S(1)} %broadcast_multiply_fusion.11) | copy-start | bytes 6148
  35.9 207.8 %copy-start.23 = (f32[512]{0:T(512)}, f32[512]{0:T(512)S(1)}, u32[]{:S(2)}) copy-start(f32[512]{0:T(512)S(1)} %add_rsqrt_fusion.3) | copy-start | bytes 6148
  35.9 7.2 %copy-start.22 = (s32[1,512]{1,0:T(1,128)S(1)}, s32[1,512]{1,0:T(1,128)}, u32[]{:S(2)}) copy-start(s32[1,512]{1,0:T(1,128)} %refs_6_.2) | copy-start | bytes 6148
  43.9 66.8 %copy-start.28 = (bf16[12]{0:T(256)(128)(2,1)S(1)}, bf16[12]{0:T(256)(128)(2,1)}, u32[]{:S(2)}) copy-start(bf16[12]{0:T(256)(128)(2,1)} %param.30) | copy-start | bytes 76
  115.6 43.0 %copy-start.1 = (f32[512,768]{1,0:T(8,128)}, f32[512,768]{1,0:T(8,128)S(1)}, u32[]{:S(2)}) copy-start(f32[512,768]{1,0:T(8,128)S(1)} %get-tuple-element.116) | copy-start | bytes 4718596
  124.3 2.6 copy-start
  146.5 19.2 %copy-start.8 = (bf16[512,3072]{1,0:T(8,128)(2,1)}, bf16[512,3072]{1,0:T(8,128)(2,1)S(1)}, u32[]{:S(2)}) copy-start(bf16[512,3072]{1,0:T(8,128)(2,1)S(1)} %get-tuple-element.117) | copy-start | bytes 9437188
  146.5 6.6 %copy-start.12 = (bf16[512,768]{1,0:T(8,128)(2,1)S(1)}, bf16[512,768]{1,0:T(8,128)(2,1)}, u32[]{:S(2)}) copy-start(bf16[512,768]{1,0:T(8,128)(2,1)} %param.23) | copy-start | bytes 2359300
  154.7 1.1 copy-start.3
  154.8 2.0 copy-start.5
  158.6 4.8 %copy-start.11 = (bf16[4,2,2,2,24,768]{5,4,3,2,1,0:T(8,128)(2,1)S(1)}, bf16[4,2,2,2,24,768]{5,4,3,2,1,0:T(8,128)(2,1)}, u32[]{:S(2)}) copy-start(bf16[4,2,2,2,24,768]{5,4,3,2,1,0:T(8,128)(2,1)} %get-tuple-element.57) | copy-start | bytes 3538948
  239.6 2.9 copy-start.10
  239.6 3.0 copy-start.13
  242.5 1.1 copy-start.9
  242.6 1.3 copy-start.7
  243.9 6.8 %copy-start.14 = (bf16[512,2304]{1,0:T(8,128)(2,1)}, bf16[512,2304]{1,0:T(8,128)(2,1)S(1)}, u32[]{:S(2)}) copy-start(bf16[512,2304]{1,0:T(8,128)(2,1)S(1)} %constant_dynamic-update-slice_fusion) | copy-start | bytes 7077892
  243.9 7.0 %copy-start.16 = (f32[64,64]{1,0:T(8,128)S(1)}, f32[64,64]{1,0:T(8,128)}, u32[]{:S(2)}) copy-start(f32[64,64]{1,0:T(8,128)} %get-tuple-element.64) | copy-start | bytes 49156
  251.8 5.8 %copy-start.15 = (bf16[512,2304]{1,0:T(8,128)(2,1)S(1)}, bf16[512,2304]{1,0:T(8,128)(2,1)}, u32[]{:S(2)}) copy-start(bf16[512,2304]{1,0:T(8,128)(2,1)} %copy-done.14) | copy-start | bytes 7077892
  257.6 4.7 %copy-start.21 = (f32[768]{0:T(1024)S(1)}, f32[768]{0:T(1024)}, u32[]{:S(2)}) copy-start(f32[768]{0:T(1024)} %get-tuple-element.118) | copy-start | bytes 9220
  263.1 40.5 %copy-start.27 = (f32[512]{0:T(512)S(1)}, f32[512]{0:T(512)}, u32[]{:S(2)}) copy-start(f32[512]{0:T(512)} %get-tuple-element.96) | copy-start | bytes 6148
  263.1 40.5 %copy-start.26 = (f32[512]{0:T(512)S(1)}, f32[512]{0:T(512)}, u32[]{:S(2)}) copy-start(f32[512]{0:T(512)} %get-tuple-element.97) | copy-start | bytes 6148
  263.1 40.5 %copy-start.4 = (f32[512,768]{1,0:T(8,128)S(1)}, f32[512,768]{1,0:T(8,128)}, u32[]{:S(2)}) copy-start(f32[512,768]{1,0:T(8,128)} %copy-done.3) | copy-start | bytes 4718596
  263.1 40.5 %copy-start.18 = (f32[512]{0:T(512)S(1)}, f32[512]{0:T(512)}, u32[]{:S(2)}) copy-start(f32[512]{0:T(512)} %copy-done.17) | copy-start | bytes 6148
  263.1 40.5 %copy-start.20 = (f32[768]{0:T(1024)S(1)}, f32[768]{0:T(1024)}, u32[]{:S(2)}) copy-start(f32[768]{0:T(1024)} %copy-done.19) | copy-start | bytes 9220
  263.1 40.5 %copy-start.24 = (f32[512]{0:T(512)S(1)}, f32[512]{0:T(512)}, u32[]{:S(2)}) copy-start(f32[512]{0:T(512)} %copy-done.23) | copy-start | bytes 6148
  303.6 3.3 %copy-start.2 = (f32[512,768]{1,0:T(8,128)S(1)}, f32[512,768]{1,0:T(8,128)}, u32[]{:S(2)}) copy-start(f32[512,768]{1,0:T(8,128)} %copy-done.1) | copy-start | bytes 4718596
